TPU v7x, 256 devices: a whole 4x4x8 slice. The times are simulated.
256 devices in a mesh: rows: 32 (over z, y), cols: 8 (over x, core).
Axes of the slice: x: 4, y: 4, z: 8, core: 2. Of those that a mesh axis runs over, the one named last changes fastest.
Arguments:
- features: bfloat16 [384, 1280, 256], P('rows', 'cols'), may hold values from -6 to 6
- weight: bfloat16 [3, 3, 256, 128], replicated, may hold values from -0.125 to 0.125
- cotangent: bfloat16 [384, 1280, 128], P('rows', 'cols'), may hold values from -6 to 6
Outputs:
- conv_out: bfloat16 [384, 1280, 128], P('rows', 'cols')
- input_grad: bfloat16 [384, 1280, 256], P('rows', 'cols')
- weight_grad: float32 [3, 3, 256, 128], replicated
All inputs are finite; a program needn't handle non-finite values.
Results may differ from a plain program's by a relative error of at most 0.001.
Values may be sent and summed in bfloat16 or wider, within the bound.
A program may use at most 64 MiB of HBM per device.

v0:
```python
import jax
import jax.numpy as jnp
from jax import lax
from jax.sharding import PartitionSpec as P

DILATION_STEP = 12


def extended(cells, sides, width):
    for axis, dim in sides:
        count = lax.axis_size(axis)
        ends = count - 1
        head = lax.slice_in_dim(cells, 0, width, axis=dim)
        tail = lax.slice_in_dim(cells, cells.shape[dim] - width, cells.shape[dim], axis=dim)
        cells = jnp.concatenate(
            [
                lax.ppermute(tail, axis, [(i, (i + 1) % count) for i in range(ends)]),
                cells,
                lax.ppermute(head, axis, [((i + 1) % count, i) for i in range(ends)]),
            ],
            axis=dim,
        )
    return cells


def window(border_padded, row_offset_tap, column_offset_tap, map_height, map_width):
    return border_padded[
        DILATION_STEP * row_offset_tap : DILATION_STEP * row_offset_tap + map_height,
        DILATION_STEP * column_offset_tap : DILATION_STEP * column_offset_tap + map_width,
    ]


def body(features, weight, cotangent):
    map_height, map_width = (features.shape[0], features.shape[1])
    cin, cout = (weight.shape[2], weight.shape[3])
    padded_feature_map = extended(features, (("rows", 0), ("cols", 1)), DILATION_STEP)
    padded_gradient_map = extended(cotangent, (("rows", 0), ("cols", 1)), DILATION_STEP)
    flat_grad = cotangent.reshape(map_height * map_width, cout)
    output = jnp.zeros((map_height * map_width, cout), jnp.float32)
    back = jnp.zeros((map_height * map_width, cin), jnp.float32)
    kernels = []
    for row_offset_tap in range(3):
        for column_offset_tap in range(3):
            tap_weight = weight[row_offset_tap, column_offset_tap]
            piece = window(
                padded_feature_map, row_offset_tap, column_offset_tap, map_height, map_width
            ).reshape(map_height * map_width, cin)
            output = output + jnp.dot(piece, tap_weight, preferred_element_type=jnp.float32)
            gpiece = window(
                padded_gradient_map,
                2 - row_offset_tap,
                2 - column_offset_tap,
                map_height,
                map_width,
            ).reshape(map_height * map_width, cout)
            back = back + jnp.dot(gpiece, tap_weight.T, preferred_element_type=jnp.float32)
            kernels.append(jnp.dot(piece.T, flat_grad, preferred_element_type=jnp.float32))
    partial_kernel = jnp.stack(kernels).reshape(3, 3, cin, cout)
    total_kernel = lax.psum(partial_kernel, ("rows", "cols"))
    pixels = map_height * lax.axis_size("rows") * map_width * lax.axis_size("cols")
    weight_grad = total_kernel * (1.0 / jnp.sqrt(jnp.float32(pixels)))
    conv_out = output.reshape(map_height, map_width, cout).astype(jnp.bfloat16)
    input_grad = back.reshape(map_height, map_width, cin).astype(jnp.bfloat16)
    return (conv_out, input_grad, weight_grad)


def solution(mesh):
    placed = (P("rows", "cols", None), P(), P("rows", "cols", None))
    return jax.shard_map(
        body,
        mesh=mesh,
        in_specs=placed,
        out_specs=(P("rows", "cols", None), P("rows", "cols", None), P()),
        check_vma=False,
    )
```

profile of v0, /device:TPU:1, one launch (start us, length us, event | category | flops | bytes accessed | tf_op | source)
XLA Modules:
  0.0 355.3 jit_solution(12603172973174778925)
XLA Ops:
  7.2 4.2 %collective-permute-start = (bf16[12,160,256]{2,1,0:T(8,128)(2,1)}, bf16[12,160,256]{2,1,0:T(8,128)(2,1)S(1)}, u32[]{:S(2)}, u32[]{:S(2)}) collective-permute-start(bf16[12,160,256]{2,1,0:T(8,128)(2,1)} %param.3), channel_id=1, source_target_pairs={{0,8},{8,16},{16,24},{24,32},{32,40},{40,48},{48,56},{56,64},{64,7... | collective-permute-start | bytes 2949128 | tf_op jit(solution)/shard_map/ppermute | solution.py:17
  11.4 1.3 collective-permute-start.1
  12.7 4.0 %collective-permute-start.4 = (bf16[12,160,128]{2,1,0:T(8,128)(2,1)}, bf16[12,160,128]{2,1,0:T(8,128)(2,1)S(1)}, u32[]{:S(2)}, u32[]{:S(2)}) collective-permute-start(bf16[12,160,128]{2,1,0:T(8,128)(2,1)} %param.5), channel_id=1, source_target_pairs={{0,8},{8,16},{16,24},{24,32},{32,40},{40,48},{48,56},{56,64},{64,7... | collective-permute-start | bytes 1474568 | tf_op jit(solution)/shard_map/ppermute | solution.py:17
  16.8 1.3 collective-permute-start.5
  18.1 1.4 fusion.37
  19.5 0.4 fusion.39
  20.0 22.7 %collective-permute-done.4 = bf16[12,160,128]{2,1,0:T(8,128)(2,1)S(1)} collective-permute-done((bf16[12,160,128]{2,1,0:T(8,128)(2,1)}, bf16[12,160,128]{2,1,0:T(8,128)(2,1)S(1)}, u32[]{:S(2)}, u32[]{:S(2)}) %collective-permute-start.4) | collective-permute-done | bytes 491552 | tf_op jit(solution)/shard_map/ppermute | solution.py:17
  42.8 3.7 %collective-permute-done.5 = bf16[12,160,128]{2,1,0:T(8,128)(2,1)S(1)} collective-permute-done((bf16[12,160,128]{2,1,0:T(8,128)(2,1)}, bf16[12,160,128]{2,1,0:T(8,128)(2,1)S(1)}, u32[]{:S(2)}, u32[]{:S(2)}) %collective-permute-start.5) | collective-permute-done | bytes 491552 | tf_op jit(solution)/shard_map/ppermute | solution.py:19
  46.6 3.7 %collective-permute-start.6 = (bf16[36,12,128]{2,1,0:T(8,128)(2,1)S(1)}, bf16[36,12,128]{2,1,0:T(8,128)(2,1)S(1)}, u32[]{:S(2)}, u32[]{:S(2)}) collective-permute-start(bf16[36,12,128]{2,1,0:T(8,128)(2,1)S(1)} %get-tuple-element.23), channel_id=1, source_target_pairs={{1,0},{2,1},{3,2},{4,3},{5,4},{6,5},{7,6},{9,8},{10,9},{11,10},{12... | collective-permute-start | bytes 331784 | tf_op jit(solution)/shard_map/ppermute | solution.py:19
  50.3 3.0 collective-permute-start.7
  53.3 0.4 fusion.49
  53.7 0.4 fusion.27
  54.2 1.2 collective-permute-done.7
  55.4 1.1 pad_maximum_fusion.8
  56.5 0.4 fusion.41
  56.9 0.4 fusion.45
  57.3 0.6 fusion.5
  58.0 0.4 fusion.23
  58.4 0.4 fusion.31
  58.8 1.7 fusion.6
  60.9 4.4 %collective-permute-start.2 = (bf16[36,12,256]{2,1,0:T(8,128)(2,1)S(1)}, bf16[36,12,256]{2,1,0:T(8,128)(2,1)S(1)}, u32[]{:S(2)}, u32[]{:S(2)}) collective-permute-start(bf16[36,12,256]{2,1,0:T(8,128)(2,1)S(1)} %get-tuple-element.12), channel_id=1, source_target_pairs={{0,1},{1,2},{2,3},{3,4},{4,5},{5,6},{6,7},{8,9},{9,10},{10,11},{11... | collective-permute-start | bytes 663560 | tf_op jit(solution)/shard_map/ppermute | solution.py:17
  65.3 2.1 collective-permute-start.3
  67.4 1.4 fusion.51
  68.7 0.4 fusion.29
  69.2 4.1 %collective-permute-done.3 = bf16[36,12,256]{2,1,0:T(8,128)(2,1)S(1)} collective-permute-done((bf16[36,12,256]{2,1,0:T(8,128)(2,1)S(1)}, bf16[36,12,256]{2,1,0:T(8,128)(2,1)S(1)}, u32[]{:S(2)}, u32[]{:S(2)}) %collective-permute-start.3) | collective-permute-done | bytes 221216 | tf_op jit(solution)/shard_map/ppermute | solution.py:19
  73.3 5.1 %pad_maximum_fusion.2 = (bf16[12,160,256]{2,1,0:T(8,128)(2,1)S(1)}, bf16[12,160,256]{2,1,0:T(8,128)(2,1)S(1)}, bf16[12,160,256]{2,1,0:T(8,128)(2,1)S(1)}, bf16[1...) fusion(bf16[36,12,256]{2,1,0:T(8,128)(2,1)S(1)} %collective-permute-done.3, ...), kind=kLoop, calls=%fused_computation.38 | loop fusion | flops 11796480 | bytes 9289728 | tf_op jit(solution)/shard_map/slice | solution.py:27
  78.5 0.5 fusion.22
  79.0 0.5 fusion.21
  79.5 0.5 fusion.20
  80.0 0.5 fusion.19
  80.5 0.5 fusion.18
  80.9 0.5 fusion.17
  81.4 0.5 fusion.16
  81.9 0.5 fusion.15
  82.4 0.5 fusion.14
  82.9 1.0 copy-done.15
  84.0 1.7 fusion.43
  85.7 0.4 fusion.47
  86.1 0.4 fusion.25
  86.6 0.4 copy-done.1
  86.9 0.3 copy-done.7
  87.2 0.5 fusion.12
  87.8 0.6 copy-done.5
  88.4 0.4 fusion.33
  88.8 0.2 copy-done.3
  89.0 1.3 fusion.13
  90.3 255.7 %all-reduce.2.cloned.1.call-done = f32[3,3,256,128]{3,2,1,0:T(8,128)} async-done(((f32[3,3,256,128]{3,2,1,0:T(8,128)}), f32[3,3,256,128]{3,2,1,0:T(8,128)}) %all-reduce.2.cloned.1.call-update) | async-done | bytes 1179664 | tf_op jit(solution)/shard_map/psum | solution.py:59
  346.1 2.4 broadcast_multiply_fusion
  (41 shorter events, 0.7 us)
Async XLA Ops:
  7.2 12.4 %copy-start = (bf16[12,160,256]{2,1,0:T(8,128)(2,1)S(1)}, bf16[12,160,256]{2,1,0:T(8,128)(2,1)}, u32[]{:S(2)}) copy-start(bf16[12,160,256]{2,1,0:T(8,128)(2,1)} %param.3) | copy-start | bytes 2949124
  7.2 12.4 %copy-start.13 = (bf16[3,3,256,128]{3,2,1,0:T(8,128)(2,1)S(1)}, bf16[3,3,256,128]{3,2,1,0:T(8,128)(2,1)}, u32[]{:S(2)}) copy-start(bf16[3,3,256,128]{3,2,1,0:T(8,128)(2,1)} %param.4) | copy-start | bytes 1769476
  7.2 338.9 %all-reduce.2.cloned.1.call-start = ((), (), s32[]{:S(2)}) async-start(), calls=%async_computation | async-start | bytes 2359296 | tf_op jit(solution)/shard_map/psum | solution.py:59
  7.2 53.3 %collective-permute-start = (bf16[12,160,256]{2,1,0:T(8,128)(2,1)}, bf16[12,160,256]{2,1,0:T(8,128)(2,1)S(1)}, u32[]{:S(2)}, u32[]{:S(2)}) collective-permute-start(bf16[12,160,256]{2,1,0:T(8,128)(2,1)} %param.3), channel_id=1, source_target_pairs={{0,8},{8,16},{16,24},{24,32},{32,40},{40,48},{48,56},{56,64},{64,7... | collective-permute-start | bytes 2949128 | tf_op jit(solution)/shard_map/ppermute | solution.py:17
  11.4 49.3 %collective-permute-start.1 = (bf16[12,160,256]{2,1,0:T(8,128)(2,1)}, bf16[12,160,256]{2,1,0:T(8,128)(2,1)S(1)}, u32[]{:S(2)}, u32[]{:S(2)}) collective-permute-start(bf16[12,160,256]{2,1,0:T(8,128)(2,1)} %param.3), channel_id=1, source_target_pairs={{8,0},{16,8},{24,16},{32,24},{40,32},{48,40},{56,48},{64,56},{72,6... | collective-permute-start | bytes 2949128 | tf_op jit(solution)/shard_map/ppermute | solution.py:19
  12.7 29.9 %collective-permute-start.4 = (bf16[12,160,128]{2,1,0:T(8,128)(2,1)}, bf16[12,160,128]{2,1,0:T(8,128)(2,1)S(1)}, u32[]{:S(2)}, u32[]{:S(2)}) collective-permute-start(bf16[12,160,128]{2,1,0:T(8,128)(2,1)} %param.5), channel_id=1, source_target_pairs={{0,8},{8,16},{16,24},{24,32},{32,40},{40,48},{48,56},{56,64},{64,7... | collective-permute-start | bytes 1474568 | tf_op jit(solution)/shard_map/ppermute | solution.py:17
  16.8 29.7 %collective-permute-start.5 = (bf16[12,160,128]{2,1,0:T(8,128)(2,1)}, bf16[12,160,128]{2,1,0:T(8,128)(2,1)S(1)}, u32[]{:S(2)}, u32[]{:S(2)}) collective-permute-start(bf16[12,160,128]{2,1,0:T(8,128)(2,1)} %param.5), channel_id=1, source_target_pairs={{8,0},{16,8},{24,16},{32,24},{40,32},{48,40},{56,48},{64,56},{72,6... | collective-permute-start | bytes 1474568 | tf_op jit(solution)/shard_map/ppermute | solution.py:19
  19.5 23.2 %copy-start.14 = (bf16[12,160,128]{2,1,0:T(8,128)(2,1)S(1)}, bf16[12,160,128]{2,1,0:T(8,128)(2,1)}, u32[]{:S(2)}) copy-start(bf16[12,160,128]{2,1,0:T(8,128)(2,1)} %param.5) | copy-start | bytes 1474564
  46.6 7.6 %collective-permute-start.6 = (bf16[36,12,128]{2,1,0:T(8,128)(2,1)S(1)}, bf16[36,12,128]{2,1,0:T(8,128)(2,1)S(1)}, u32[]{:S(2)}, u32[]{:S(2)}) collective-permute-start(bf16[36,12,128]{2,1,0:T(8,128)(2,1)S(1)} %get-tuple-element.23), channel_id=1, source_target_pairs={{1,0},{2,1},{3,2},{4,3},{5,4},{6,5},{7,6},{9,8},{10,9},{11,10},{12... | collective-permute-start | bytes 331784 | tf_op jit(solution)/shard_map/ppermute | solution.py:19
  50.3 5.1 %collective-permute-start.7 = (bf16[36,12,128]{2,1,0:T(8,128)(2,1)S(1)}, bf16[36,12,128]{2,1,0:T(8,128)(2,1)S(1)}, u32[]{:S(2)}, u32[]{:S(2)}) collective-permute-start(bf16[36,12,128]{2,1,0:T(8,128)(2,1)S(1)} %get-tuple-element.24), channel_id=1, source_target_pairs={{0,1},{1,2},{2,3},{3,4},{4,5},{5,6},{6,7},{8,9},{9,10},{10,11},{11... | collective-permute-start | bytes 331784 | tf_op jit(solution)/shard_map/ppermute | solution.py:17
  60.9 8.3 %collective-permute-start.2 = (bf16[36,12,256]{2,1,0:T(8,128)(2,1)S(1)}, bf16[36,12,256]{2,1,0:T(8,128)(2,1)S(1)}, u32[]{:S(2)}, u32[]{:S(2)}) collective-permute-start(bf16[36,12,256]{2,1,0:T(8,128)(2,1)S(1)} %get-tuple-element.12), channel_id=1, source_target_pairs={{0,1},{1,2},{2,3},{3,4},{4,5},{5,6},{6,7},{8,9},{9,10},{10,11},{11... | collective-permute-start | bytes 663560 | tf_op jit(solution)/shard_map/ppermute | solution.py:17
  65.3 8.0 %collective-permute-start.3 = (bf16[36,12,256]{2,1,0:T(8,128)(2,1)S(1)}, bf16[36,12,256]{2,1,0:T(8,128)(2,1)S(1)}, u32[]{:S(2)}, u32[]{:S(2)}) collective-permute-start(bf16[36,12,256]{2,1,0:T(8,128)(2,1)S(1)} %get-tuple-element.13), channel_id=1, source_target_pairs={{1,0},{2,1},{3,2},{4,3},{5,4},{6,5},{7,6},{9,8},{10,9},{11,10},{12... | collective-permute-start | bytes 663560 | tf_op jit(solution)/shard_map/ppermute | solution.py:19
  78.5 1.5 copy-start.6
  78.5 1.5 copy-start.10
  78.5 2.5 copy-start.2
  78.5 2.9 copy-start.4
  78.5 3.9 %copy-start.12 = (bf16[12,160,256]{2,1,0:T(8,128)(2,1)}, bf16[12,160,256]{2,1,0:T(8,128)(2,1)S(1)}, u32[]{:S(2)}) copy-start(bf16[12,160,256]{2,1,0:T(8,128)(2,1)S(1)} %get-tuple-element.10) | copy-start | bytes 2949124
  78.5 3.9 %copy-start.8 = (bf16[12,160,256]{2,1,0:T(8,128)(2,1)}, bf16[12,160,256]{2,1,0:T(8,128)(2,1)S(1)}, u32[]{:S(2)}) copy-start(bf16[12,160,256]{2,1,0:T(8,128)(2,1)S(1)} %get-tuple-element.5) | copy-start | bytes 2949124
  82.9 1.0 copy-start.15
  83.9 1.8 copy-start.11
  83.9 2.2 copy-start.9
  85.7 1.2 copy-start.1
  85.7 1.5 copy-start.7
  87.2 1.2 copy-start.5
  87.8 1.3 copy-start.3
Sparse Core Ops, SparseCore 0:
  84.1 261.9 all-reduce.1
where the time goes:
time: 358 us; the launch traced here: 355 us
  waiting for transfers between devices  287 us (80%)
  starting transfers between devices  24.1 us (7%)
  matrix products  17.5 us (5%)
  between operations  14.5 us (4%)
  other arithmetic  8.62 us (2%)
    psum x1, waiting for transfers between devices, body(): total_kernel = lax.psum(partial_kernel, ('rows', 'cols'))  256 us
    ppermute x4, waiting for transfers between devices, extended(): lax.ppermute(tail, axis, [(i, (i + 1) % count) for i in range(ends)])  23.9 us
    ppermute x4, starting transfers between devices, extended(): lax.ppermute(tail, axis, [(i, (i + 1) % count) for i in range(ends)])  15.6 us
    ppermute x4, starting transfers between devices, extended(): lax.ppermute(head, axis, [((i + 1) % count, i) for i in range(ends)])  8.4 us
    ppermute x4, waiting for transfers between devices, extended(): lax.ppermute(head, axis, [((i + 1) % count, i) for i in range(ends)])  7.85 us
  transfers between devices with their start and end apart: 9, of which 5 were waited for; matrix products, arithmetic and copies ran while one was open for 4% of the time, Pallas kernels for 0%

commit v1 on v0

--- a/solution.py
+++ b/solution.py
@@ -1,9 +1,263 @@
+import functools
+
 import jax
 import jax.numpy as jnp
 from jax import lax
+from jax.experimental import pallas as pl
+from jax.experimental.pallas import tpu as pltpu
 from jax.sharding import PartitionSpec as P
 
 DILATION_STEP = 12
+MESH = pl.DeviceIdType.MESH
+NX, NY, NZ = 4, 4, 8
+HALF, SHARD, PART = 384, 96, 16
+
+
+def position():
+    row, col = lax.axis_index("rows"), lax.axis_index("cols")
+    return row, col, lax.div(col, 2), lax.rem(col, 2), lax.rem(row, NY), lax.div(row, NY)
+
+
+def z_offset(z):
+    return pl.multiple_of(lax.div(3 * z, 2) * 8, 8)
+
+
+def rows_at(start, size):
+    return pl.ds(pl.multiple_of(start, 8), size)
+
+
+class Reduction:
+    def __init__(self, piece, where, partial, total, scratch):
+        self.k = piece
+        self.row, self.col, self.x, self.core, self.y, self.z = where
+        (self.half, self.s1, self.xs, self.s2, self.zs, self.ys, self.zg, self.xg_own, self.near, self.xsem, self.zsem, self.ysem,
+         self.zgsem, self.xgsem, self.farsem) = scratch
+        self.partial, self.total = partial, total
+
+    def copy(self, src, dst, sems, to):
+        return pltpu.make_async_remote_copy(
+            src_ref=src, dst_ref=dst, send_sem=sems[0], recv_sem=sems[1], device_id=to, device_id_type=MESH
+        )
+
+    def partner(self):
+        return (self.row, self.x * 2 + 1 - self.core)
+
+    def x_peer(self, d):
+        return (self.row, lax.rem(self.x + d, NX) * 2 + self.core)
+
+    def y_peer(self, d):
+        return (self.z * NY + lax.rem(self.y + d, NY), self.col)
+
+    def z_peer(self, d):
+        return (lax.rem(self.z + d, NZ) * NY + self.y, self.col)
+
+    def core_copy(self):
+        k = self.k
+        return self.copy(
+            self.partial.at[k, rows_at((1 - self.core) * HALF, HALF)], self.half.at[k], (self.near.at[0, k], self.near.at[1, k]),
+            self.partner(),
+        )
+
+    def x_copy(self, d):
+        k = self.k
+        target = lax.rem(self.x + d, NX)
+        return self.copy(
+            self.s1.at[k, rows_at(target * SHARD, SHARD)], self.xs.at[k, d - 1], (self.xsem.at[0, k, d - 1], self.xsem.at[1, k, d - 1]),
+            self.x_peer(d),
+        )
+
+    def z_copy(self, d):
+        k = self.k
+        target = lax.rem(self.z + d, NZ)
+        return self.copy(
+            self.s2.at[k, pl.ds(z_offset(target), PART)], self.zs.at[k, d - 1], (self.zsem.at[0, k, d - 1], self.zsem.at[1, k, d - 1]),
+            self.z_peer(d),
+        )
+
+    def y_copy(self, d):
+        k = self.k
+        return self.copy(
+            self.ys.at[k, self.y], self.ys.at[k, self.y], (self.ysem.at[0, k, d - 1], self.ysem.at[1, k, d - 1]), self.y_peer(d)
+        )
+
+    def zg_copy(self, d):
+        k = self.k
+        return self.copy(
+            self.zg.at[k, self.z], self.zg.at[k, self.z], (self.zgsem.at[0, k, d - 1], self.zgsem.at[1, k, d - 1]), self.z_peer(d)
+        )
+
+    def span(self, x):
+        return rows_at(self.core * HALF + x * SHARD, SHARD)
+
+    def xg_copy(self, d):
+        k = self.k
+        return self.copy(
+            self.total.at[k, self.span(self.x)], self.total.at[k, self.span(self.x)],
+            (self.xgsem.at[0, k, d - 1], self.xgsem.at[1, k, d - 1]), self.x_peer(d),
+        )
+
+    def far_copy(self, d):
+        k = self.k
+        span = self.span(lax.rem(self.x + NX - d, NX))
+        return self.copy(
+            self.total.at[k, span], self.total.at[k, span], (self.farsem.at[0, k, d], self.farsem.at[1, k, d]), self.partner()
+        )
+
+    def loop(self, n, body):
+        def step(d, carry):
+            body(d)
+            return carry
+
+        lax.fori_loop(1, n, step, 0)
+
+    def to_core(self):
+        self.core_copy().start()
+
+    def to_x(self):
+        k = self.k
+        self.core_copy().wait_recv()
+        self.s1[k] = self.partial[k, rows_at(self.core * HALF, HALF)] + self.half[k]
+        for d in (1, 3, 2):
+            self.x_copy(d).start()
+
+    def to_z(self):
+        k = self.k
+        for d in range(1, NX):
+            self.x_copy(d).wait_recv()
+        self.s2[k] = self.s1[k, rows_at(self.x * SHARD, SHARD)] + self.xs[k, 0] + self.xs[k, 1] + self.xs[k, 2]
+        self.loop(NZ, lambda d: self.z_copy(d).start())
+
+    def to_y(self):
+        k = self.k
+        self.loop(NZ, lambda d: self.z_copy(d).wait_recv())
+        mine = self.s2[k, pl.ds(z_offset(self.z), PART)]
+        for d in range(NZ - 1):
+            mine = mine + self.zs[k, d]
+        self.ys[k, self.y] = mine
+        for d in range(1, NY):
+            self.y_copy(d).start()
+
+    def gather_z(self, scale):
+        k = self.k
+        for d in range(1, NY):
+            self.y_copy(d).wait_recv()
+        self.zg[k, self.z] = (self.ys[k, 0] + self.ys[k, 1] + self.ys[k, 2] + self.ys[k, 3]) * scale
+        self.loop(NZ, lambda d: self.zg_copy(d).start())
+
+    def gather_x(self):
+        k = self.k
+        self.loop(NZ, lambda d: self.zg_copy(d).wait_recv())
+        base = self.core * HALF + self.x * SHARD
+        for pair in range(NZ // 2):
+            self.total[k, rows_at(base + 24 * pair, 16)] = self.zg[k, 2 * pair]
+            self.total[k, rows_at(base + 24 * pair + 16, 8)] = self.zg[k, 2 * pair + 1, 8:16]
+        for d in (1, 3, 2):
+            self.xg_copy(d).start()
+        self.far_copy(0).start()
+
+    def gather_core(self):
+        for d in (1, 3, 2):
+            self.xg_copy(d).wait_recv()
+            self.far_copy(d).start()
+
+    def finish(self):
+        for d in range(NX):
+            self.far_copy(d).wait_recv()
+
+    def drain(self):
+        self.core_copy().wait_send()
+        for d in range(1, NX):
+            self.x_copy(d).wait_send()
+            self.xg_copy(d).wait_send()
+        self.loop(NZ, lambda d: self.z_copy(d).wait_send())
+        self.loop(NZ, lambda d: self.zg_copy(d).wait_send())
+        for d in range(1, NY):
+            self.y_copy(d).wait_send()
+        for d in range(NX):
+            self.far_copy(d).wait_send()
+
+
+def reduction_scratch(pieces):
+    f32 = jnp.float32
+    dma = pltpu.SemaphoreType.DMA
+    return [
+        pltpu.VMEM((pieces, HALF, 128), f32),
+        pltpu.VMEM((pieces, HALF, 128), f32),
+        pltpu.VMEM((pieces, NX - 1, SHARD, 128), f32),
+        pltpu.VMEM((pieces, SHARD, 128), f32),
+        pltpu.VMEM((pieces, NZ - 1, PART, 128), f32),
+        pltpu.VMEM((pieces, NY, PART, 128), f32),
+        pltpu.VMEM((pieces, NZ, PART, 128), f32),
+        pltpu.VMEM((8, 128), f32),
+        dma((2, pieces)),
+        dma((2, pieces, NX - 1)),
+        dma((2, pieces, NZ - 1)),
+        dma((2, pieces, NY - 1)),
+        dma((2, pieces, NZ - 1)),
+        dma((2, pieces, NX - 1)),
+        dma((2, pieces, NX)),
+    ]
+
+
+def greet(where, extra=()):
+    row, col, x, core, y, z = where
+    barrier = pltpu.get_barrier_semaphore()
+
+    def signal(to):
+        pl.semaphore_signal(barrier, inc=1, device_id=to, device_id_type=MESH)
+
+    count = 0
+    for to in extra:
+        signal(to)
+        count += 1
+    signal((row, x * 2 + 1 - core))
+    for d in range(1, NX):
+        signal((row, lax.rem(x + d, NX) * 2 + core))
+    for d in range(1, NY):
+        signal((z * NY + lax.rem(y + d, NY), col))
+
+    def step(d, carry):
+        signal((lax.rem(z + d, NZ) * NY + y, col))
+        return carry
+
+    lax.fori_loop(1, NZ, step, 0)
+    pl.semaphore_wait(barrier, count + 1 + NX - 1 + NY - 1 + NZ - 1)
+
+
+def reduce_kernel(scale, partial, total, *scratch):
+    where = position()
+    greet(where)
+    pieces = [Reduction(k, where, partial, total, scratch) for k in range(3)]
+    for p in pieces:
+        p.to_core()
+    for p in pieces:
+        p.to_x()
+    for p in pieces:
+        p.to_z()
+    for p in pieces:
+        p.to_y()
+    for p in pieces:
+        p.gather_z(scale)
+    for p in pieces:
+        p.gather_x()
+    for p in pieces:
+        p.gather_core()
+    for p in pieces:
+        p.finish()
+    for p in pieces:
+        p.drain()
+
+
+def reduced(partial, scale):
+    return pl.pallas_call(
+        functools.partial(reduce_kernel, scale),
+        out_shape=jax.ShapeDtypeStruct((3, 768, 128), jnp.float32),
+        in_specs=[pl.BlockSpec(memory_space=pltpu.VMEM)],
+        out_specs=pl.BlockSpec(memory_space=pltpu.VMEM),
+        scratch_shapes=reduction_scratch(3),
+        compiler_params=pltpu.CompilerParams(collective_id=0, has_side_effects=True),
+        name="reduce_kernel",
+    )(partial)
 
 
 def extended(cells, sides, width):
@@ -55,10 +309,9 @@
             ).reshape(map_height * map_width, cout)
             back = back + jnp.dot(gpiece, tap_weight.T, preferred_element_type=jnp.float32)
             kernels.append(jnp.dot(piece.T, flat_grad, preferred_element_type=jnp.float32))
-    partial_kernel = jnp.stack(kernels).reshape(3, 3, cin, cout)
-    total_kernel = lax.psum(partial_kernel, ("rows", "cols"))
+    partial_kernel = jnp.stack(kernels).reshape(3, 3 * cin, cout)
     pixels = map_height * lax.axis_size("rows") * map_width * lax.axis_size("cols")
-    weight_grad = total_kernel * (1.0 / jnp.sqrt(jnp.float32(pixels)))
+    weight_grad = reduced(partial_kernel, float(pixels) ** -0.5).reshape(3, 3, cin, cout)
     conv_out = output.reshape(map_height, map_width, cout).astype(jnp.bfloat16)
     input_grad = back.reshape(map_height, map_width, cin).astype(jnp.bfloat16)
     return (conv_out, input_grad, weight_grad)

time: 358 us -> 130 us (0.36)
  waiting for transfers between devices: 287 us -> 32.7 us
  Pallas kernels: 0 us -> 43.1 us
  between operations: 14.5 us -> 1.09 us
    psum x1 -> x0, waiting for transfers between devices: 256 us -> none  [body(): total_kernel = lax.psum(partial_kernel, ('rows', 'cols'))]
    pallas_call x0 -> x1, Pallas kernels: none -> 43.1 us  [reduced(): pl.pallas_call(functools.partial(reduce_kernel, scale), out_shape=jax.Sha...]
  transfers between devices with their start and end apart: 9 -> 8, of which waited for: 5 -> 6; matrix products, arithmetic and copies ran while one was open for 4% -> 7% of each run, Pallas kernels for 0% -> 0%
where the time goes in v1:
time: 130 us; the launch traced here: 129 us
  Pallas kernels  43.1 us (33%)
  waiting for transfers between devices  32.7 us (25%)
  starting transfers between devices  24 us (18%)
  matrix products  17.7 us (14%)
  other arithmetic  6.99 us (5%)
  local copies, waits for them, and re-layouts  3.72 us (3%)
    pallas_call x1, Pallas kernels, reduced(): pl.pallas_call(functools.partial(reduce_kernel, scale), out_shape=jax.Sha...  43.1 us
    ppermute x4, waiting for transfers between devices, extended(): lax.ppermute(tail, axis, [(i, (i + 1) % count) for i in range(ends)])  24.6 us
    ppermute x4, starting transfers between devices, extended(): lax.ppermute(tail, axis, [(i, (i + 1) % count) for i in range(ends)])  15.6 us
    ppermute x4, starting transfers between devices, extended(): lax.ppermute(head, axis, [((i + 1) % count, i) for i in range(ends)])  8.4 us
    ppermute x4, waiting for transfers between devices, extended(): lax.ppermute(head, axis, [((i + 1) % count, i) for i in range(ends)])  8.13 us
    slice x2, other arithmetic, window(): border_padded[DILATION_STEP * row_offset_tap:DILATION_STEP * row_offset_t...  6.99 us
    dot_general x9, matrix products, body(): jnp.dot(gpiece, tap_weight.T, preferred_element_type=jnp.float32)  6.17 us
    dot_general x9, matrix products, body(): jnp.dot(piece, tap_weight, preferred_element_type=jnp.float32)  5.94 us
  transfers between devices with their start and end apart: 8, of which 6 were waited for; matrix products, arithmetic and copies ran while one was open for 7% of the time, Pallas kernels for 0%

profile of v1, /device:TPU:1, one launch (start us, length us, event | category | flops | bytes accessed | tf_op | source)
XLA Modules:
  0.0 129.4 jit_solution(7549667876524256814)
XLA Ops:
  0.6 4.2 %collective-permute-start = (bf16[12,160,256]{2,1,0:T(8,128)(2,1)}, bf16[12,160,256]{2,1,0:T(8,128)(2,1)S(1)}, u32[]{:S(2)}, u32[]{:S(2)}) collective-permute-start(bf16[12,160,256]{2,1,0:T(8,128)(2,1)} %param.3), channel_id=1, source_target_pairs={{0,8},{8,16},{16,24},{24,32},{32,40},{40,48},{48,56},{56,64},{64,7... | collective-permute-start | bytes 2949128 | tf_op jit(solution)/shard_map/ppermute | solution.py:271
  4.9 1.3 collective-permute-start.1
  6.2 4.0 %collective-permute-start.4 = (bf16[12,160,128]{2,1,0:T(8,128)(2,1)}, bf16[12,160,128]{2,1,0:T(8,128)(2,1)S(1)}, u32[]{:S(2)}, u32[]{:S(2)}) collective-permute-start(bf16[12,160,128]{2,1,0:T(8,128)(2,1)} %param.5), channel_id=1, source_target_pairs={{0,8},{8,16},{16,24},{24,32},{32,40},{40,48},{48,56},{56,64},{64,7... | collective-permute-start | bytes 1474568 | tf_op jit(solution)/shard_map/ppermute | solution.py:271
  10.2 1.3 collective-permute-start.5
  11.5 1.4 %fusion.37 = f32[1920,256]{1,0:T(8,128)S(1)} fusion(bf16[1920,128]{1,0:T(8,128)(2,1)} %bitcast.157, bf16[3,3,256,128]{3,2,1,0:T(8,128)(2,1)} %param.4), kind=kOutput, calls=%fused_computation.62 | convolution fusion | flops 125829120 | bytes 2523136 | tf_op jit(solution)/shard_map/dot_general | solution.py:310
  13.0 0.4 fusion.39
  13.4 22.7 %collective-permute-done.4 = bf16[12,160,128]{2,1,0:T(8,128)(2,1)S(1)} collective-permute-done((bf16[12,160,128]{2,1,0:T(8,128)(2,1)}, bf16[12,160,128]{2,1,0:T(8,128)(2,1)S(1)}, u32[]{:S(2)}, u32[]{:S(2)}) %collective-permute-start.4) | collective-permute-done | bytes 491552 | tf_op jit(solution)/shard_map/ppermute | solution.py:271
  36.2 3.7 %collective-permute-done.5 = bf16[12,160,128]{2,1,0:T(8,128)(2,1)S(1)} collective-permute-done((bf16[12,160,128]{2,1,0:T(8,128)(2,1)}, bf16[12,160,128]{2,1,0:T(8,128)(2,1)S(1)}, u32[]{:S(2)}, u32[]{:S(2)}) %collective-permute-start.5) | collective-permute-done | bytes 491552 | tf_op jit(solution)/shard_map/ppermute | solution.py:273
  40.0 3.7 %collective-permute-start.6 = (bf16[36,12,128]{2,1,0:T(8,128)(2,1)S(1)}, bf16[36,12,128]{2,1,0:T(8,128)(2,1)S(1)}, u32[]{:S(2)}, u32[]{:S(2)}) collective-permute-start(bf16[36,12,128]{2,1,0:T(8,128)(2,1)S(1)} %get-tuple-element.23), channel_id=1, source_target_pairs={{1,0},{2,1},{3,2},{4,3},{5,4},{6,5},{7,6},{9,8},{10,9},{11,10},{12... | collective-permute-start | bytes 331784 | tf_op jit(solution)/shard_map/ppermute | solution.py:273
  43.7 3.0 %collective-permute-start.7 = (bf16[36,12,128]{2,1,0:T(8,128)(2,1)S(1)}, bf16[36,12,128]{2,1,0:T(8,128)(2,1)S(1)}, u32[]{:S(2)}, u32[]{:S(2)}) collective-permute-start(bf16[36,12,128]{2,1,0:T(8,128)(2,1)S(1)} %get-tuple-element.24), channel_id=1, source_target_pairs={{0,1},{1,2},{2,3},{3,4},{4,5},{5,6},{6,7},{8,9},{9,10},{10,11},{11... | collective-permute-start | bytes 331784 | tf_op jit(solution)/shard_map/ppermute | solution.py:271
  46.7 0.4 fusion.49
  47.2 0.4 fusion.27
  47.6 1.2 collective-permute-done.7
  48.8 1.1 pad_maximum_fusion.8
  49.9 0.4 fusion.41
  50.3 0.4 fusion.45
  50.7 0.6 fusion.5
  51.4 0.4 fusion.23
  51.8 0.4 fusion.31
  52.2 1.6 %fusion.6 = bf16[1920,256]{1,0:T(8,128)(2,1)} fusion(f32[1920,256]{1,0:T(8,128)S(1)} %fusion.23, f32[1920,256]{1,0:T(8,128)S(1)} %fusion.27, f32[1920,256]{1,0:T(8,128)S(1)} %fusion.31, f32[1920,256]{1,0:T(8,128)S(1)} %fusion.5, bf16[1920,128]{1,0:T(8,128)(2,1)S(1)} %bitcast.164, bf16[3,3,256,128]{3,2,1,0:T(8,128)(2,1)S(1)} %copy-done.12), kind=kOutput, calls=%fused_computation.8 | convolution fusion | flops 128286720 | bytes 9404416 | tf_op jit(solution)/shard_map/dot_general | solution.py:310
  54.2 4.4 %collective-permute-start.2 = (bf16[36,12,256]{2,1,0:T(8,128)(2,1)S(1)}, bf16[36,12,256]{2,1,0:T(8,128)(2,1)S(1)}, u32[]{:S(2)}, u32[]{:S(2)}) collective-permute-start(bf16[36,12,256]{2,1,0:T(8,128)(2,1)S(1)} %get-tuple-element.12), channel_id=1, source_target_pairs={{0,1},{1,2},{2,3},{3,4},{4,5},{5,6},{6,7},{8,9},{9,10},{10,11},{11... | collective-permute-start | bytes 663560 | tf_op jit(solution)/shard_map/ppermute | solution.py:271
  58.6 2.1 %collective-permute-start.3 = (bf16[36,12,256]{2,1,0:T(8,128)(2,1)S(1)}, bf16[36,12,256]{2,1,0:T(8,128)(2,1)S(1)}, u32[]{:S(2)}, u32[]{:S(2)}) collective-permute-start(bf16[36,12,256]{2,1,0:T(8,128)(2,1)S(1)} %get-tuple-element.13), channel_id=1, source_target_pairs={{1,0},{2,1},{3,2},{4,3},{5,4},{6,5},{7,6},{9,8},{10,9},{11,10},{12... | collective-permute-start | bytes 663560 | tf_op jit(solution)/shard_map/ppermute | solution.py:273
  60.7 0.4 fusion.51
  61.1 0.4 fusion.29
  61.5 0.7 collective-permute-done.2
  62.2 4.4 %collective-permute-done.3 = bf16[36,12,256]{2,1,0:T(8,128)(2,1)S(1)} collective-permute-done((bf16[36,12,256]{2,1,0:T(8,128)(2,1)S(1)}, bf16[36,12,256]{2,1,0:T(8,128)(2,1)S(1)}, u32[]{:S(2)}, u32[]{:S(2)}) %collective-permute-start.3) | collective-permute-done | bytes 221216 | tf_op jit(solution)/shard_map/ppermute | solution.py:273
  66.6 5.9 %pad_maximum_fusion.2 = (bf16[12,160,256]{2,1,0:T(8,128)(2,1)S(1)}, bf16[12,160,256]{2,1,0:T(8,128)(2,1)S(1)}, bf16[12,160,256]{2,1,0:T(8,128)(2,1)S(1)}, bf16[1...) fusion(bf16[36,12,256]{2,1,0:T(8,128)(2,1)S(1)} %collective-permute-done.3, ...), kind=kLoop, calls=%fused_computation.38 | loop fusion | flops 11796480 | bytes 9289728 | tf_op jit(solution)/shard_map/slice | solution.py:281
  72.5 0.5 fusion.22
  73.0 0.5 fusion.21
  73.5 0.5 fusion.20
  74.0 1.9 %fusion.19 = f32[9,256,128]{2,1,0:T(8,128)S(1)} fusion(f32[9,256,128]{2,1,0:T(8,128)S(1)} %fusion.20, bf16[12,160,256]{2,1,0:T(8,128)(2,1)} %get-tuple-element.10, bf16[12,160,128]{2,1,0:T(8,128)(2,1)S(1)} %copy-done.13), kind=kOutput, calls=%fused_computation.29 | convolution fusion | flops 125829120 | bytes 1605632 | tf_op jit(solution)/shard_map/dot_general | solution.py:311
  75.8 0.5 fusion.18
  76.3 0.5 fusion.17
  76.8 0.5 fusion.16
  77.3 0.5 fusion.15
  77.8 0.5 fusion.14
  78.3 1.0 copy-done.14
  79.3 43.1 %reduce_kernel.1 = f32[3,768,128]{2,1,0:T(8,128)} custom-call(f32[3,768,128]{2,1,0:T(8,128)} %bitcast.166), custom_call_target="tpu_custom_call" | custom-call | tf_op jit(solution)/shard_map/reduce_kernel/pallas_call | solution.py:252
  122.4 1.7 %fusion.43 = f32[1920,128]{1,0:T(8,128)S(1)} fusion(bf16[1920,256]{1,0:T(8,128)(2,1)} %bitcast.6, bf16[3,3,256,128]{3,2,1,0:T(8,128)(2,1)S(1)} %copy-done.12), kind=kOutput, calls=%fused_computation.68 | convolution fusion | flops 125829120 | bytes 2031616 | tf_op jit(solution)/shard_map/dot_general | solution.py:302
  124.2 0.4 fusion.47
  124.6 0.4 fusion.25
  125.1 0.3 copy-done.7
  125.4 0.4 fusion.33
  125.8 0.1 copy-done.5
  125.9 0.5 fusion.12
  126.4 0.7 copy-done.3
  127.1 1.3 fusion.13
  128.4 1.0 copy.19
  (37 shorter events, 0.6 us)
Async XLA Ops:
  0.6 12.3 %copy-start.1 = (bf16[12,160,256]{2,1,0:T(8,128)(2,1)S(1)}, bf16[12,160,256]{2,1,0:T(8,128)(2,1)}, u32[]{:S(2)}) copy-start(bf16[12,160,256]{2,1,0:T(8,128)(2,1)} %param.3) | copy-start | bytes 2949124
  0.6 12.3 %copy-start.12 = (bf16[3,3,256,128]{3,2,1,0:T(8,128)(2,1)S(1)}, bf16[3,3,256,128]{3,2,1,0:T(8,128)(2,1)}, u32[]{:S(2)}) copy-start(bf16[3,3,256,128]{3,2,1,0:T(8,128)(2,1)} %param.4) | copy-start | bytes 1769476
  0.6 53.2 %collective-permute-start = (bf16[12,160,256]{2,1,0:T(8,128)(2,1)}, bf16[12,160,256]{2,1,0:T(8,128)(2,1)S(1)}, u32[]{:S(2)}, u32[]{:S(2)}) collective-permute-start(bf16[12,160,256]{2,1,0:T(8,128)(2,1)} %param.3), channel_id=1, source_target_pairs={{0,8},{8,16},{16,24},{24,32},{32,40},{40,48},{48,56},{56,64},{64,7... | collective-permute-start | bytes 2949128 | tf_op jit(solution)/shard_map/ppermute | solution.py:271
  4.9 49.1 %collective-permute-start.1 = (bf16[12,160,256]{2,1,0:T(8,128)(2,1)}, bf16[12,160,256]{2,1,0:T(8,128)(2,1)S(1)}, u32[]{:S(2)}, u32[]{:S(2)}) collective-permute-start(bf16[12,160,256]{2,1,0:T(8,128)(2,1)} %param.3), channel_id=1, source_target_pairs={{8,0},{16,8},{24,16},{32,24},{40,32},{48,40},{56,48},{64,56},{72,6... | collective-permute-start | bytes 2949128 | tf_op jit(solution)/shard_map/ppermute | solution.py:273
  6.2 29.9 %collective-permute-start.4 = (bf16[12,160,128]{2,1,0:T(8,128)(2,1)}, bf16[12,160,128]{2,1,0:T(8,128)(2,1)S(1)}, u32[]{:S(2)}, u32[]{:S(2)}) collective-permute-start(bf16[12,160,128]{2,1,0:T(8,128)(2,1)} %param.5), channel_id=1, source_target_pairs={{0,8},{8,16},{16,24},{24,32},{32,40},{40,48},{48,56},{56,64},{64,7... | collective-permute-start | bytes 1474568 | tf_op jit(solution)/shard_map/ppermute | solution.py:271
  10.2 29.7 %collective-permute-start.5 = (bf16[12,160,128]{2,1,0:T(8,128)(2,1)}, bf16[12,160,128]{2,1,0:T(8,128)(2,1)S(1)}, u32[]{:S(2)}, u32[]{:S(2)}) collective-permute-start(bf16[12,160,128]{2,1,0:T(8,128)(2,1)} %param.5), channel_id=1, source_target_pairs={{8,0},{16,8},{24,16},{32,24},{40,32},{48,40},{56,48},{64,56},{72,6... | collective-permute-start | bytes 1474568 | tf_op jit(solution)/shard_map/ppermute | solution.py:273
  12.9 23.2 %copy-start.13 = (bf16[12,160,128]{2,1,0:T(8,128)(2,1)S(1)}, bf16[12,160,128]{2,1,0:T(8,128)(2,1)}, u32[]{:S(2)}) copy-start(bf16[12,160,128]{2,1,0:T(8,128)(2,1)} %param.5) | copy-start | bytes 1474564
  40.0 7.6 %collective-permute-start.6 = (bf16[36,12,128]{2,1,0:T(8,128)(2,1)S(1)}, bf16[36,12,128]{2,1,0:T(8,128)(2,1)S(1)}, u32[]{:S(2)}, u32[]{:S(2)}) collective-permute-start(bf16[36,12,128]{2,1,0:T(8,128)(2,1)S(1)} %get-tuple-element.23), channel_id=1, source_target_pairs={{1,0},{2,1},{3,2},{4,3},{5,4},{6,5},{7,6},{9,8},{10,9},{11,10},{12... | collective-permute-start | bytes 331784 | tf_op jit(solution)/shard_map/ppermute | solution.py:273
  43.7 5.1 %collective-permute-start.7 = (bf16[36,12,128]{2,1,0:T(8,128)(2,1)S(1)}, bf16[36,12,128]{2,1,0:T(8,128)(2,1)S(1)}, u32[]{:S(2)}, u32[]{:S(2)}) collective-permute-start(bf16[36,12,128]{2,1,0:T(8,128)(2,1)S(1)} %get-tuple-element.24), channel_id=1, source_target_pairs={{0,1},{1,2},{2,3},{3,4},{4,5},{5,6},{6,7},{8,9},{9,10},{10,11},{11... | collective-permute-start | bytes 331784 | tf_op jit(solution)/shard_map/ppermute | solution.py:271
  54.2 8.0 %collective-permute-start.2 = (bf16[36,12,256]{2,1,0:T(8,128)(2,1)S(1)}, bf16[36,12,256]{2,1,0:T(8,128)(2,1)S(1)}, u32[]{:S(2)}, u32[]{:S(2)}) collective-permute-start(bf16[36,12,256]{2,1,0:T(8,128)(2,1)S(1)} %get-tuple-element.12), channel_id=1, source_target_pairs={{0,1},{1,2},{2,3},{3,4},{4,5},{5,6},{6,7},{8,9},{9,10},{10,11},{11... | collective-permute-start | bytes 663560 | tf_op jit(solution)/shard_map/ppermute | solution.py:271
  58.6 8.0 %collective-permute-start.3 = (bf16[36,12,256]{2,1,0:T(8,128)(2,1)S(1)}, bf16[36,12,256]{2,1,0:T(8,128)(2,1)S(1)}, u32[]{:S(2)}, u32[]{:S(2)}) collective-permute-start(bf16[36,12,256]{2,1,0:T(8,128)(2,1)S(1)} %get-tuple-element.13), channel_id=1, source_target_pairs={{1,0},{2,1},{3,2},{4,3},{5,4},{6,5},{7,6},{9,8},{10,9},{11,10},{12... | collective-permute-start | bytes 663560 | tf_op jit(solution)/shard_map/ppermute | solution.py:273
  72.5 1.5 %copy-start.4 = (bf16[12,160,256]{2,1,0:T(8,128)(2,1)}, bf16[12,160,256]{2,1,0:T(8,128)(2,1)S(1)}, u32[]{:S(2)}) copy-start(bf16[12,160,256]{2,1,0:T(8,128)(2,1)S(1)} %get-tuple-element.11) | copy-start | bytes 2949124
  72.5 1.5 %copy-start.10 = (bf16[12,160,256]{2,1,0:T(8,128)(2,1)}, bf16[12,160,256]{2,1,0:T(8,128)(2,1)S(1)}, u32[]{:S(2)}) copy-start(bf16[12,160,256]{2,1,0:T(8,128)(2,1)S(1)} %get-tuple-element.4) | copy-start | bytes 2949124
  72.5 3.8 %copy-start.2 = (bf16[12,160,256]{2,1,0:T(8,128)(2,1)}, bf16[12,160,256]{2,1,0:T(8,128)(2,1)S(1)}, u32[]{:S(2)}) copy-start(bf16[12,160,256]{2,1,0:T(8,128)(2,1)S(1)} %get-tuple-element.3) | copy-start | bytes 2949124
  72.5 4.3 %copy-start.6 = (bf16[12,160,256]{2,1,0:T(8,128)(2,1)}, bf16[12,160,256]{2,1,0:T(8,128)(2,1)S(1)}, u32[]{:S(2)}) copy-start(bf16[12,160,256]{2,1,0:T(8,128)(2,1)S(1)} %get-tuple-element.9) | copy-start | bytes 2949124
  72.5 5.3 %copy-start.8 = (bf16[12,160,256]{2,1,0:T(8,128)(2,1)}, bf16[12,160,256]{2,1,0:T(8,128)(2,1)S(1)}, u32[]{:S(2)}) copy-start(bf16[12,160,256]{2,1,0:T(8,128)(2,1)S(1)} %get-tuple-element.5) | copy-start | bytes 2949124
  78.3 1.0 copy-start.14
  122.4 1.8 %copy-start.11 = (bf16[12,160,256]{2,1,0:T(8,128)(2,1)S(1)}, bf16[12,160,256]{2,1,0:T(8,128)(2,1)}, u32[]{:S(2)}) copy-start(bf16[12,160,256]{2,1,0:T(8,128)(2,1)} %copy-done.10) | copy-start | bytes 2949124
  122.4 2.2 %copy-start.9 = (bf16[12,160,256]{2,1,0:T(8,128)(2,1)S(1)}, bf16[12,160,256]{2,1,0:T(8,128)(2,1)}, u32[]{:S(2)}) copy-start(bf16[12,160,256]{2,1,0:T(8,128)(2,1)} %copy-done.8) | copy-start | bytes 2949124
  124.2 1.2 copy-start.7
  124.6 1.3 copy-start.5
  125.9 1.2 copy-start.3
  127.1 1.3 copy-start

commit v2 on v1

--- a/solution.py
+++ b/solution.py
@@ -7,7 +7,9 @@
 from jax.experimental.pallas import tpu as pltpu
 from jax.sharding import PartitionSpec as P
 
-DILATION_STEP = 12
+ROWS = 12
+BLOCKS, COLS = 32, 8
+F_CHUNKS, G_CHUNKS = 4, 2
 MESH = pl.DeviceIdType.MESH
 NX, NY, NZ = 4, 4, 8
 HALF, SHARD, PART = 384, 96, 16
@@ -224,97 +226,279 @@
     pl.semaphore_wait(barrier, count + 1 + NX - 1 + NY - 1 + NZ - 1)
 
 
-def reduce_kernel(scale, partial, total, *scratch):
+class Halo:
+    def __init__(self, buf, where, strip_sem, row_sem, relay_sem, chunks):
+        self.buf = buf
+        self.row, self.col = where[0], where[1]
+        self.strip_sem, self.row_sem, self.relay_sem = strip_sem, row_sem, relay_sem
+        self.chunks = chunks
+        self.n = ROWS // chunks
+
+    def beside(self, side):
+        step = 1 if side == 1 else COLS - 1
+        return (self.row, lax.rem(self.col + step, COLS))
+
+    def beyond(self, way):
+        step = 1 if way == 0 else BLOCKS - 1
+        return (lax.rem(self.row + step, BLOCKS), self.col)
+
+    def edge(self, side):
+        return (pl.ds(160, 16), pl.ds(0, 16)) if side == 1 else (pl.ds(16, 16), pl.ds(176, 16))
+
+    def copy(self, src, dst, send, recv, to):
+        return pltpu.make_async_remote_copy(
+            src_ref=src, dst_ref=dst, send_sem=send, recv_sem=recv, device_id=to, device_id_type=MESH
+        )
+
+    def strip(self, side):
+        here, there = self.edge(side)
+        rows = pl.ds(ROWS, ROWS)
+        return self.copy(
+            self.buf.at[rows, here, :], self.buf.at[rows, there, :], self.strip_sem.at[0, side], self.strip_sem.at[1, side],
+            self.beside(side),
+        )
+
+    def block(self, way, j):
+        src = pl.ds(ROWS + j * self.n, self.n)
+        dst = pl.ds((0 if way == 0 else 2 * ROWS) + j * self.n, self.n)
+        mid = pl.ds(16, 160)
+        return self.copy(
+            self.buf.at[src, mid, :], self.buf.at[dst, mid, :], self.row_sem.at[0, way, j], self.row_sem.at[1, way, j], self.beyond(way)
+        )
+
+    def relay(self, way, side, j):
+        here, there = self.edge(side)
+        rows = pl.ds((0 if way == 0 else 2 * ROWS) + j * self.n, self.n)
+        return self.copy(
+            self.buf.at[rows, here, :], self.buf.at[rows, there, :], self.relay_sem.at[0, way, side, j],
+            self.relay_sem.at[1, way, side, j], self.beside(side),
+        )
+
+    def take(self, way, j):
+        self.block(way, j).wait_recv()
+        self.relay(way, 0, j).start()
+        self.relay(way, 1, j).start()
+
+    def took(self, way, j):
+        self.relay(way, 0, j).wait_recv()
+        self.relay(way, 1, j).wait_recv()
+
+    def blank_columns(self, first, n):
+        zeros = jnp.zeros((n, 16, self.buf.shape[2]), self.buf.dtype)
+
+        @pl.when(self.col == 0)
+        def _():
+            self.buf[first : first + n, 0:16, :] = zeros
+
+        @pl.when(self.col == COLS - 1)
+        def _():
+            self.buf[first : first + n, 176:192, :] = zeros
+
+    def unfold(self, into, first, n, inside=None):
+        c = self.buf.shape[2]
+        self.blank_columns(first, n)
+
+        def shift():
+            def body(i, carry):
+                r = first + i
+                into[r, :, 0:c] = self.buf[r, 4:164, :]
+                into[r, :, c : 2 * c] = self.buf[r, 16:176, :]
+                into[r, :, 2 * c : 3 * c] = self.buf[r, 28:188, :]
+                return carry
+
+            lax.fori_loop(0, n, body, 0)
+
+        if inside is None:
+            shift()
+            return
+        pl.when(inside)(shift)
+
+        @pl.when(jnp.logical_not(inside))
+        def _():
+            def body(i, carry):
+                into[first + i] = jnp.zeros((160, 3 * c), into.dtype)
+                return carry
+
+            lax.fori_loop(0, n, body, 0)
+
+    def drain(self):
+        for side in range(2):
+            self.strip(side).wait_send()
+        for way in range(2):
+            for j in range(self.chunks):
+                self.block(way, j).wait_send()
+                for side in range(2):
+                    self.relay(way, side, j).wait_send()
+
+
+def branch_kernel(scale, f_hbm, w_hbm, g_hbm, out, back, total, *scratch):
+    (fx, gx, fim, gim, ft, w, w9, acc, partial, load_sem, f_strip, f_row, f_relay, g_strip, g_row, g_relay) = scratch[:16]
     where = position()
-    greet(where)
-    pieces = [Reduction(k, where, partial, total, scratch) for k in range(3)]
-    for p in pieces:
-        p.to_core()
-    for p in pieces:
-        p.to_x()
-    for p in pieces:
-        p.to_z()
-    for p in pieces:
-        p.to_y()
-    for p in pieces:
-        p.gather_z(scale)
-    for p in pieces:
-        p.gather_x()
-    for p in pieces:
-        p.gather_core()
-    for p in pieces:
-        p.finish()
-    for p in pieces:
-        p.drain()
-
-
-def reduced(partial, scale):
-    return pl.pallas_call(
-        functools.partial(reduce_kernel, scale),
-        out_shape=jax.ShapeDtypeStruct((3, 768, 128), jnp.float32),
-        in_specs=[pl.BlockSpec(memory_space=pltpu.VMEM)],
-        out_specs=pl.BlockSpec(memory_space=pltpu.VMEM),
-        scratch_shapes=reduction_scratch(3),
-        compiler_params=pltpu.CompilerParams(collective_id=0, has_side_effects=True),
-        name="reduce_kernel",
-    )(partial)
-
-
-def extended(cells, sides, width):
-    for axis, dim in sides:
-        count = lax.axis_size(axis)
-        ends = count - 1
-        head = lax.slice_in_dim(cells, 0, width, axis=dim)
-        tail = lax.slice_in_dim(cells, cells.shape[dim] - width, cells.shape[dim], axis=dim)
-        cells = jnp.concatenate(
-            [
-                lax.ppermute(tail, axis, [(i, (i + 1) % count) for i in range(ends)]),
-                cells,
-                lax.ppermute(head, axis, [((i + 1) % count, i) for i in range(ends)]),
-            ],
-            axis=dim,
-        )
-    return cells
-
-
-def window(border_padded, row_offset_tap, column_offset_tap, map_height, map_width):
-    return border_padded[
-        DILATION_STEP * row_offset_tap : DILATION_STEP * row_offset_tap + map_height,
-        DILATION_STEP * column_offset_tap : DILATION_STEP * column_offset_tap + map_width,
-    ]
+    row, col = where[0], where[1]
+    mine = pl.ds(ROWS, ROWS)
+    g_load = pltpu.make_async_copy(g_hbm, gx.at[mine, pl.ds(16, 160), :], load_sem.at[0])
+    f_load = pltpu.make_async_copy(f_hbm, fx.at[mine, pl.ds(16, 160), :], load_sem.at[1])
+    w_load = pltpu.make_async_copy(w_hbm, w, load_sem.at[2])
+    g_load.start()
+    f_load.start()
+    w_load.start()
+    f = Halo(fx, where, f_strip, f_row, f_relay, F_CHUNKS)
+    g = Halo(gx, where, g_strip, g_row, g_relay, G_CHUNKS)
+    red = [Reduction(k, where, partial, total, scratch[16:]) for k in range(3)]
+    greet(where, (f.beside(0), f.beside(1), f.beyond(0), f.beyond(1)))
+
+    g_load.wait()
+    g.strip(0).start()
+    g.strip(1).start()
+    for j in range(G_CHUNKS):
+        for way in range(2):
+            g.block(way, j).start()
+    f_load.wait()
+    f.strip(0).start()
+    f.strip(1).start()
+
+    for i in range(3):
+        ft[:, 640 * i : 640 * (i + 1)] = fx[ROWS + 4 * i : ROWS + 4 * (i + 1), 16:176, :].reshape(640, 256).T
+    w_load.wait()
+    for kb in range(3):
+        for si in range(3):
+            at = (3 * kb + si) * 128
+            w9[:, at : at + 128] = w[2 - kb, 2 - si]
+
+    above, below = row > 0, row < BLOCKS - 1
+
+    def kernel_gradient(kb):
+        pairs = gim[kb * ROWS : (kb + 1) * ROWS].reshape(ROWS * 160, 384)
+        products = jnp.dot(ft[...], pairs, preferred_element_type=jnp.float32)
+        for si in range(3):
+            partial[2 - kb, (2 - si) * 256 : (3 - si) * 256, :] = products[:, si * 128 : (si + 1) * 128]
+        red[2 - kb].to_core()
+
+    def convolve(kb, first, n):
+        piece = fim[kb * ROWS + first : kb * ROWS + first + n].reshape(n * 160, 768)
+        return jnp.dot(piece, w[kb].reshape(768, 128), preferred_element_type=jnp.float32)
+
+    def input_gradient(i):
+        n = 4
+        piece = jnp.concatenate(
+            [gim[kb * ROWS + n * i : kb * ROWS + n * (i + 1)].reshape(n * 160, 384) for kb in range(3)], axis=1
+        )
+        grad = lax.dot_general(piece, w9[...], (((1,), (1,)), ((), ())), preferred_element_type=jnp.float32)
+        back[n * i : n * (i + 1)] = grad.astype(back.dtype).reshape(n, 160, 256)
+
+    g.strip(0).wait_recv()
+    g.strip(1).wait_recv()
+    g.unfold(gim, ROWS, ROWS)
+    kernel_gradient(1)
+    for j in range(F_CHUNKS):
+        for way in range(2):
+            f.block(way, j).start()
+
+    f.strip(0).wait_recv()
+    f.strip(1).wait_recv()
+    f.unfold(fim, ROWS, ROWS)
+    for i in range(3):
+        acc[i * 640 : (i + 1) * 640, :] = convolve(1, 4 * i, 4)
+    red[1].to_x()
+    for j in range(G_CHUNKS):
+        for way in range(2):
+            g.take(way, j)
+    red[1].to_z()
+    for way, kb, inside in ((0, 0, above), (1, 2, below)):
+        for j in range(G_CHUNKS):
+            g.took(way, j)
+        g.unfold(gim, kb * ROWS, ROWS, inside)
+        kernel_gradient(kb)
+
+    red[1].to_y()
+    red[2].to_x()
+    red[0].to_x()
+    input_gradient(0)
+    red[1].gather_z(scale)
+    input_gradient(1)
+    red[2].to_z()
+    red[0].to_z()
+    input_gradient(2)
+    red[1].gather_x()
+    red[2].to_y()
+    red[0].to_y()
+    red[1].gather_core()
+
+    def features_taken(j):
+        f.take(0, j)
+        f.take(1, j)
+
+    def features_used(j):
+        n = ROWS // F_CHUNKS
+        first = n * j
+        f.took(0, j)
+        f.took(1, j)
+        f.unfold(fim, first, n, above)
+        f.unfold(fim, 2 * ROWS + first, n, below)
+        at = first * 160
+        value = acc[at : at + n * 160, :] + convolve(0, first, n) + convolve(2, first, n)
+        out[first : first + n] = value.astype(out.dtype).reshape(n, 160, 128)
+
+    features_taken(0)
+    features_taken(1)
+    features_used(0)
+    red[2].gather_z(scale)
+    red[0].gather_z(scale)
+    features_taken(2)
+    features_used(1)
+    red[2].gather_x()
+    red[0].gather_x()
+    features_taken(3)
+    features_used(2)
+    features_used(3)
+    red[2].gather_core()
+    red[0].gather_core()
+    for k in (1, 2, 0):
+        red[k].finish()
+    for k in (1, 2, 0):
+        red[k].drain()
+    g.drain()
+    f.drain()
 
 
 def body(features, weight, cotangent):
-    map_height, map_width = (features.shape[0], features.shape[1])
-    cin, cout = (weight.shape[2], weight.shape[3])
-    padded_feature_map = extended(features, (("rows", 0), ("cols", 1)), DILATION_STEP)
-    padded_gradient_map = extended(cotangent, (("rows", 0), ("cols", 1)), DILATION_STEP)
-    flat_grad = cotangent.reshape(map_height * map_width, cout)
-    output = jnp.zeros((map_height * map_width, cout), jnp.float32)
-    back = jnp.zeros((map_height * map_width, cin), jnp.float32)
-    kernels = []
-    for row_offset_tap in range(3):
-        for column_offset_tap in range(3):
-            tap_weight = weight[row_offset_tap, column_offset_tap]
-            piece = window(
-                padded_feature_map, row_offset_tap, column_offset_tap, map_height, map_width
-            ).reshape(map_height * map_width, cin)
-            output = output + jnp.dot(piece, tap_weight, preferred_element_type=jnp.float32)
-            gpiece = window(
-                padded_gradient_map,
-                2 - row_offset_tap,
-                2 - column_offset_tap,
-                map_height,
-                map_width,
-            ).reshape(map_height * map_width, cout)
-            back = back + jnp.dot(gpiece, tap_weight.T, preferred_element_type=jnp.float32)
-            kernels.append(jnp.dot(piece.T, flat_grad, preferred_element_type=jnp.float32))
-    partial_kernel = jnp.stack(kernels).reshape(3, 3 * cin, cout)
-    pixels = map_height * lax.axis_size("rows") * map_width * lax.axis_size("cols")
-    weight_grad = reduced(partial_kernel, float(pixels) ** -0.5).reshape(3, 3, cin, cout)
-    conv_out = output.reshape(map_height, map_width, cout).astype(jnp.bfloat16)
-    input_grad = back.reshape(map_height, map_width, cin).astype(jnp.bfloat16)
-    return (conv_out, input_grad, weight_grad)
+    bf16, f32 = jnp.bfloat16, jnp.float32
+    dma = pltpu.SemaphoreType.DMA
+    pixels = ROWS * BLOCKS * 160 * COLS
+    anywhere = pl.BlockSpec(memory_space=pl.ANY)
+    vmem = pl.BlockSpec(memory_space=pltpu.VMEM)
+    conv_out, input_grad, weight_grad = pl.pallas_call(
+        functools.partial(branch_kernel, float(pixels) ** -0.5),
+        out_shape=(
+            jax.ShapeDtypeStruct((ROWS, 160, 128), bf16),
+            jax.ShapeDtypeStruct((ROWS, 160, 256), bf16),
+            jax.ShapeDtypeStruct((3, 768, 128), f32),
+        ),
+        in_specs=[anywhere] * 3,
+        out_specs=(vmem, vmem, vmem),
+        scratch_shapes=[
+            pltpu.VMEM((3 * ROWS, 192, 256), bf16),
+            pltpu.VMEM((3 * ROWS, 192, 128), bf16),
+            pltpu.VMEM((3 * ROWS, 160, 768), bf16),
+            pltpu.VMEM((3 * ROWS, 160, 384), bf16),
+            pltpu.VMEM((256, ROWS * 160), bf16),
+            pltpu.VMEM((3, 3, 256, 128), bf16),
+            pltpu.VMEM((256, 1152), bf16),
+            pltpu.VMEM((ROWS * 160, 128), f32),
+            pltpu.VMEM((3, 768, 128), f32),
+            dma((3,)),
+            dma((2, 2)),
+            dma((2, 2, F_CHUNKS)),
+            dma((2, 2, 2, F_CHUNKS)),
+            dma((2, 2)),
+            dma((2, 2, G_CHUNKS)),
+            dma((2, 2, 2, G_CHUNKS)),
+        ]
+        + reduction_scratch(3),
+        compiler_params=pltpu.CompilerParams(collective_id=0, has_side_effects=True, vmem_limit_bytes=60 * 1024 * 1024),
+        name="branch_kernel",
+    )(features, weight, cotangent)
+    return conv_out, input_grad, weight_grad.reshape(weight.shape)
 
 
 def solution(mesh):

time: 130 us -> 85.7 us (0.66)
  Pallas kernels: 43.1 us -> 80.3 us
  waiting for transfers between devices: 32.7 us -> 0 us
  starting transfers between devices: 24 us -> 0 us
  matrix products: 17.7 us -> 0 us
  other arithmetic: 6.99 us -> 0 us
    pallas_call x1, Pallas kernels: 43.1 us -> 80.3 us  [body(): pl.pallas_call(functools.partial(branch_kernel, float(pixels) ** (-0.5)),...]
    ppermute x8 -> x0, waiting for transfers between devices: 32.7 us -> none  [the longest x4 24.6 us: extended(): lax.ppermute(tail, axis, [(i, (i + 1) % count) for i in range(ends)])]
    ppermute x8 -> x0, starting transfers between devices: 24 us -> none  [the longest x4 15.6 us: extended(): lax.ppermute(tail, axis, [(i, (i + 1) % count) for i in range(ends)])]
    dot_general x27 -> x0, matrix products: 17.7 us -> none  [the longest x9 6.17 us: body(): jnp.dot(gpiece, tap_weight.T, preferred_element_type=jnp.float32)]
    slice x2 -> x0, other arithmetic: 6.99 us -> none  [window(): border_padded[DILATION_STEP * row_offset_tap:DILATION_STEP * row_offset_t...]
    unnamed x35 -> x7, local copies, waits for them, and re-layouts: 3.45 us -> 4.57 us
  transfers between devices with their start and end apart: 8 -> 0, of which waited for: 6 -> 0; matrix products, arithmetic and copies ran while one was open for 7% -> 0% of each run, Pallas kernels for 0% -> 0%
where the time goes in v2:
time: 85.7 us; the launch traced here: 85.6 us
  Pallas kernels  80.3 us (94%)
  local copies, waits for them, and re-layouts  4.57 us (5%)
    pallas_call x1, Pallas kernels, body(): pl.pallas_call(functools.partial(branch_kernel, float(pixels) ** (-0.5)),...  80.3 us
    unnamed x7, local copies, waits for them, and re-layouts  4.57 us

profile of v2, /device:TPU:1, one launch (start us, length us, event | category | flops | bytes accessed | tf_op | source)
XLA Modules:
  0.0 85.6 jit_solution(17222267098300711394)
XLA Ops:
  0.6 80.3 %branch_kernel.1 = (bf16[12,160,128]{2,1,0:T(8,128)(2,1)}, bf16[12,160,256]{2,1,0:T(8,128)(2,1)}, f32[3,768,128]{2,1,0:T(8,128)}) custom-call(bf16[12,160,256]{2,1,0:T(8,128)(2,1)} %f_hbm.1, bf16[3,3,256,128]{3,2,1,0:T(8,128)(2,1)} %w_hbm.1, bf16[12,160,128]{2,1,0:T(8,128)(2,1)} %g_hbm.1), custom_call_target="tpu_custom_call" | custom-call | tf_op jit(solution)/shard_map/branch_kernel/pallas_call | solution.py:470
  81.0 0.0 copy-start.1
  81.0 1.9 %copy.9 = bf16[12,160,128]{2,1,0:T(8,128)(2,1)} copy(bf16[12,160,128]{2,1,0:T(8,128)(2,1)} %get-tuple-element.12) | data formatting | bytes 983040
  82.9 0.0 copy-done.1
  82.9 0.0 copy-start
  82.9 0.9 %copy.10 = bf16[12,160,256]{2,1,0:T(8,128)(2,1)} copy(bf16[12,160,256]{2,1,0:T(8,128)(2,1)S(1)} %copy-done.1) | data formatting | bytes 1966080
  83.9 0.7 copy-done
  84.5 1.0 %copy.11 = f32[3,3,256,128]{3,2,1,0:T(8,128)} copy(f32[3,3,256,128]{3,2,1,0:T(8,128)S(1)} %bitcast.1) | data formatting | bytes 2359296
Async XLA Ops:
  81.0 1.9 %copy-start.1 = (bf16[12,160,256]{2,1,0:T(8,128)(2,1)S(1)}, bf16[12,160,256]{2,1,0:T(8,128)(2,1)}, u32[]{:S(2)}) copy-start(bf16[12,160,256]{2,1,0:T(8,128)(2,1)} %get-tuple-element.13) | copy-start | bytes 2949124
  82.9 1.6 %copy-start = (f32[3,768,128]{2,1,0:T(8,128)S(1)}, f32[3,768,128]{2,1,0:T(8,128)}, u32[]{:S(2)}) copy-start(f32[3,768,128]{2,1,0:T(8,128)} %get-tuple-element.8) | copy-start | bytes 3538948

commit v3 on v2

v3 whole, which is shorter than its diff:
```python
import functools

import jax
import jax.numpy as jnp
from jax import lax
from jax.experimental import pallas as pl
from jax.experimental.pallas import tpu as pltpu
from jax.sharding import PartitionSpec as P

ROWS = 12
BLOCKS, COLS = 32, 8
G_SIZES, F_SIZES = (4, 4, 4), (2, 3, 2, 2, 3)
G_DIRECT, F_DIRECT = 1, 0
VMEM_BYTES = 36 * 1024 * 1024
MESH = pl.DeviceIdType.MESH
NX, NY, NZ = 4, 4, 8
HALF, PART = 384, 16


def position():
    row, col = lax.axis_index("rows"), lax.axis_index("cols")
    return row, col, lax.div(col, 2), lax.rem(col, 2), lax.rem(row, NY), lax.div(row, NY)


def part_offset(i):
    return pl.multiple_of(lax.div(3 * i, 2) * 8, 8)


def rows_at(start, size):
    return pl.ds(pl.multiple_of(start, 8), size)


class Reduction:
    def __init__(self, piece, order, where, partial, total, scratch):
        self.k = piece
        self.row, self.col, self.x, self.core, self.y, self.z = where
        (self.half, self.s1, self.first, self.s2, self.second, self.ys, self.parts, self.near, self.first_sem, self.second_sem,
         self.ysem, self.parts_sem, self.whole_sem, self.far_sem) = scratch
        self.partial, self.total = partial, total
        self.order = order
        self.n1, self.n2 = (NX, NZ) if order == "xz" else (NZ, NX)
        self.i1, self.i2 = (self.x, self.z) if order == "xz" else (self.z, self.x)
        self.shard = HALF // self.n1

    def copy(self, src, dst, sems, slot, to):
        return pltpu.make_async_remote_copy(
            src_ref=src, dst_ref=dst, send_sem=sems.at[0, self.k, slot], recv_sem=sems.at[1, self.k, slot], device_id=to,
            device_id_type=MESH,
        )

    def partner(self):
        return (self.row, self.x * 2 + 1 - self.core)

    def along(self, axis, d):
        if axis == "x":
            return (self.row, lax.rem(self.x + d, NX) * 2 + self.core)
        if axis == "y":
            return (self.z * NY + lax.rem(self.y + d, NY), self.col)
        return (lax.rem(self.z + d, NZ) * NY + self.y, self.col)

    def core_copy(self):
        k = self.k
        return self.copy(self.partial.at[k, rows_at((1 - self.core) * HALF, HALF)], self.half.at[k], self.near, 0, self.partner())

    def first_copy(self, d):
        k = self.k
        target = lax.rem(self.i1 + d, self.n1)
        return self.copy(
            self.s1.at[k, rows_at(target * self.shard, self.shard)], self.first.at[k, d - 1, pl.ds(0, self.shard)], self.first_sem,
            d - 1, self.along(self.order[0], d),
        )

    def second_copy(self, d):
        k = self.k
        target = lax.rem(self.i2 + d, self.n2)
        return self.copy(
            self.s2.at[k, pl.ds(part_offset(target), PART)], self.second.at[k, d - 1], self.second_sem, d - 1,
            self.along(self.order[1], d),
        )

    def y_copy(self, d):
        return self.copy(self.ys.at[self.k, self.y], self.ys.at[self.k, self.y], self.ysem, d - 1, self.along("y", d))

    def part_copy(self, d):
        here = self.parts.at[self.k, self.i2]
        return self.copy(here, here, self.parts_sem, d - 1, self.along(self.order[1], d))

    def span(self, i):
        return self.total.at[self.k, rows_at(self.core * HALF + i * self.shard, self.shard)]

    def whole_copy(self, d):
        here = self.span(self.i1)
        return self.copy(here, here, self.whole_sem, d - 1, self.along(self.order[0], d))

    def far_copy(self, d):
        here = self.span(lax.rem(self.i1 + self.n1 - d, self.n1))
        return self.copy(here, here, self.far_sem, d, self.partner())

    def loop(self, n, body, start=1):
        if n <= 4:
            for d in range(start, n):
                body(d)
            return

        def step(d, carry):
            body(d)
            return carry

        lax.fori_loop(start, n, step, 0)

    def to_core(self):
        self.core_copy().start()

    def to_first(self):
        k = self.k
        self.core_copy().wait_recv()
        self.s1[k] = self.partial[k, rows_at(self.core * HALF, HALF)] + self.half[k]
        self.loop(self.n1, lambda d: self.first_copy(d).start())

    def to_second(self):
        k, n = self.k, self.shard
        self.loop(self.n1, lambda d: self.first_copy(d).wait_recv())
        value = self.s1[k, rows_at(self.i1 * n, n)]
        for d in range(self.n1 - 1):
            value = value + self.first[k, d, 0:n]
        self.s2[k, 0:n] = value
        self.loop(self.n2, lambda d: self.second_copy(d).start())

    def to_y(self):
        k = self.k
        self.loop(self.n2, lambda d: self.second_copy(d).wait_recv())
        mine = self.s2[k, pl.ds(part_offset(self.i2), PART)]
        for d in range(self.n2 - 1):
            mine = mine + self.second[k, d]
        self.ys[k, self.y] = mine
        for d in range(1, NY):
            self.y_copy(d).start()

    def gather_parts(self, scale):
        k = self.k
        for d in range(1, NY):
            self.y_copy(d).wait_recv()
        self.parts[k, self.i2] = (self.ys[k, 0] + self.ys[k, 1] + self.ys[k, 2] + self.ys[k, 3]) * scale
        self.loop(self.n2, lambda d: self.part_copy(d).start())

    def gather_whole(self):
        k = self.k
        self.loop(self.n2, lambda d: self.part_copy(d).wait_recv())
        base = self.core * HALF + self.i1 * self.shard
        for pair in range(self.n2 // 2):
            self.total[k, rows_at(base + 24 * pair, 16)] = self.parts[k, 2 * pair]
            self.total[k, rows_at(base + 24 * pair + 16, 8)] = self.parts[k, 2 * pair + 1, 8:16]
        self.loop(self.n1, lambda d: self.whole_copy(d).start())
        self.far_copy(0).start()

    def gather_core(self):
        def hand_on(d):
            self.whole_copy(d).wait_recv()
            self.far_copy(d).start()

        self.loop(self.n1, hand_on)

    def finish(self):
        self.loop(self.n1, lambda d: self.far_copy(d).wait_recv(), 0)

    def drain(self):
        self.core_copy().wait_send()
        self.loop(self.n1, lambda d: self.first_copy(d).wait_send())
        self.loop(self.n1, lambda d: self.whole_copy(d).wait_send())
        self.loop(self.n2, lambda d: self.second_copy(d).wait_send())
        self.loop(self.n2, lambda d: self.part_copy(d).wait_send())
        for d in range(1, NY):
            self.y_copy(d).wait_send()
        self.loop(self.n1, lambda d: self.far_copy(d).wait_send(), 0)


def reduction_scratch(pieces):
    f32 = jnp.float32
    dma = pltpu.SemaphoreType.DMA
    most = max(NX, NZ)
    return [
        pltpu.VMEM((pieces, HALF, 128), f32),
        pltpu.VMEM((pieces, HALF, 128), f32),
        pltpu.VMEM((pieces, most - 1, HALF // NX, 128), f32),
        pltpu.VMEM((pieces, HALF // NX, 128), f32),
        pltpu.VMEM((pieces, most - 1, PART, 128), f32),
        pltpu.VMEM((pieces, NY, PART, 128), f32),
        pltpu.VMEM((pieces, most, PART, 128), f32),
        dma((2, pieces, 1)),
        dma((2, pieces, most - 1)),
        dma((2, pieces, most - 1)),
        dma((2, pieces, NY - 1)),
        dma((2, pieces, most - 1)),
        dma((2, pieces, most - 1)),
        dma((2, pieces, most)),
    ]


def greet(where, extra=()):
    row, col, x, core, y, z = where
    barrier = pltpu.get_barrier_semaphore()

    def signal(to):
        pl.semaphore_signal(barrier, inc=1, device_id=to, device_id_type=MESH)

    count = 0
    for to in extra:
        signal(to)
        count += 1
    signal((row, x * 2 + 1 - core))
    for d in range(1, NX):
        signal((row, lax.rem(x + d, NX) * 2 + core))
    for d in range(1, NY):
        signal((z * NY + lax.rem(y + d, NY), col))

    def step(d, carry):
        signal((lax.rem(z + d, NZ) * NY + y, col))
        return carry

    lax.fori_loop(1, NZ, step, 0)
    pl.semaphore_wait(barrier, count + 1 + NX - 1 + NY - 1 + NZ - 1)


class Halo:
    def __init__(self, buf, where, strip_sem, row_sem, relay_sem, sizes, direct=0):
        self.buf = buf
        self.row, self.col = where[0], where[1]
        self.strip_sem, self.row_sem, self.relay_sem = strip_sem, row_sem, relay_sem
        self.sizes = sizes
        self.starts = [sum(sizes[:j]) for j in range(len(sizes))]
        self.chunks = len(sizes)
        self.relayed = self.chunks - direct

    def beside(self, side):
        step = 1 if side == 1 else COLS - 1
        return (self.row, lax.rem(self.col + step, COLS))

    def beyond(self, way):
        step = 1 if way == 0 else BLOCKS - 1
        return (lax.rem(self.row + step, BLOCKS), self.col)

    def edge(self, side):
        return (pl.ds(160, 16), pl.ds(0, 16)) if side == 1 else (pl.ds(16, 16), pl.ds(176, 16))

    def copy(self, src, dst, send, recv, to):
        return pltpu.make_async_remote_copy(
            src_ref=src, dst_ref=dst, send_sem=send, recv_sem=recv, device_id=to, device_id_type=MESH
        )

    def strip(self, side):
        here, there = self.edge(side)
        rows = pl.ds(ROWS, ROWS)
        return self.copy(
            self.buf.at[rows, here, :], self.buf.at[rows, there, :], self.strip_sem.at[0, side], self.strip_sem.at[1, side],
            self.beside(side),
        )

    def block(self, way, j):
        src = pl.ds(ROWS + self.starts[j], self.sizes[j])
        dst = pl.ds((0 if way == 0 else 2 * ROWS) + self.starts[j], self.sizes[j])
        mid = pl.ds(16, 160)
        return self.copy(
            self.buf.at[src, mid, :], self.buf.at[dst, mid, :], self.row_sem.at[0, way, j], self.row_sem.at[1, way, j], self.beyond(way)
        )

    def relay(self, way, side, j):
        here, there = self.edge(side)
        rows = pl.ds((0 if way == 0 else 2 * ROWS) + self.starts[j], self.sizes[j])
        source, to = rows, self.beside(side)
        if j >= self.relayed:
            source, to = pl.ds(ROWS + self.starts[j], self.sizes[j]), (self.beyond(way)[0], self.beside(side)[1])
        return self.copy(
            self.buf.at[source, here, :], self.buf.at[rows, there, :], self.relay_sem.at[0, way, side, j],
            self.relay_sem.at[1, way, side, j], to,
        )

    def send(self, j):
        if j >= self.relayed:
            for way in range(2):
                for side in range(2):
                    self.relay(way, side, j).start()
        for way in range(2):
            self.block(way, j).start()

    def corners(self):
        return [(self.beyond(way)[0], self.beside(side)[1]) for way in range(2) for side in range(2)]

    def take(self, way, j):
        self.block(way, j).wait_recv()
        if j < self.relayed:
            self.relay(way, 0, j).start()
            self.relay(way, 1, j).start()

    def took(self, way, j):
        self.relay(way, 0, j).wait_recv()
        self.relay(way, 1, j).wait_recv()

    def blank_columns(self, first, n):
        zeros = jnp.zeros((n, 16, self.buf.shape[2]), self.buf.dtype)

        @pl.when(self.col == 0)
        def _():
            self.buf[first : first + n, 0:16, :] = zeros

        @pl.when(self.col == COLS - 1)
        def _():
            self.buf[first : first + n, 176:192, :] = zeros

    def unfold(self, into, first, n, inside=None):
        c = self.buf.shape[2]
        self.blank_columns(first, n)

        def shift():
            def body(i, carry):
                r = first + i
                into[r, :, 0:c] = self.buf[r, 4:164, :]
                into[r, :, c : 2 * c] = self.buf[r, 16:176, :]
                into[r, :, 2 * c : 3 * c] = self.buf[r, 28:188, :]
                return carry

            lax.fori_loop(0, n, body, 0)

        if inside is None:
            shift()
            return
        pl.when(inside)(shift)

        @pl.when(jnp.logical_not(inside))
        def _():
            def body(i, carry):
                into[first + i] = jnp.zeros((160, 3 * c), into.dtype)
                return carry

            lax.fori_loop(0, n, body, 0)

    def drain(self):
        for side in range(2):
            self.strip(side).wait_send()
        for way in range(2):
            for j in range(self.chunks):
                self.block(way, j).wait_send()
                for side in range(2):
                    self.relay(way, side, j).wait_send()


def branch_kernel(scale, f_hbm, w_hbm, g_hbm, out, back, total, *scratch):
    (fx, gx, fim, gim, ft, w, w9, acc, partial, load_sem, f_strip, f_row, f_relay, g_strip, g_row, g_relay) = scratch[:16]
    where = position()
    row, col = where[0], where[1]
    mine = pl.ds(ROWS, ROWS)
    g_load = pltpu.make_async_copy(g_hbm, gx.at[mine, pl.ds(16, 160), :], load_sem.at[0])
    f_load = pltpu.make_async_copy(f_hbm, fx.at[mine, pl.ds(16, 160), :], load_sem.at[1])
    w_load = pltpu.make_async_copy(w_hbm, w, load_sem.at[2])
    g_load.start()
    f_load.start()
    w_load.start()
    f = Halo(fx, where, f_strip, f_row, f_relay, F_SIZES, F_DIRECT)
    g = Halo(gx, where, g_strip, g_row, g_relay, G_SIZES, G_DIRECT)
    red = [Reduction(k, order, where, partial, total, scratch[16:]) for k, order in enumerate(("xz", "xz", "xz"))]
    greet(where, (f.beside(0), f.beside(1), f.beyond(0), f.beyond(1), *(g.corners() if G_DIRECT + F_DIRECT else ())))

    g_load.wait()
    g.strip(0).start()
    g.strip(1).start()
    for j in range(len(G_SIZES)):
        g.send(j)
    f_load.wait()
    f.strip(0).start()
    f.strip(1).start()
    f.send(0)

    for i in range(3):
        ft[:, 640 * i : 640 * (i + 1)] = fx[ROWS + 4 * i : ROWS + 4 * (i + 1), 16:176, :].reshape(640, 256).T
    w_load.wait()
    for kb in range(3):
        for si in range(3):
            at = (3 * kb + si) * 128
            w9[:, at : at + 128] = w[2 - kb, 2 - si]

    above, below = row > 0, row < BLOCKS - 1

    def kernel_gradient(kb, i):
        pairs = gim[kb * ROWS + 4 * i : kb * ROWS + 4 * (i + 1)].reshape(640, 384)
        products = jnp.dot(ft[:, 640 * i : 640 * (i + 1)], pairs, preferred_element_type=jnp.float32)
        for si in range(3):
            tap = products[:, si * 128 : (si + 1) * 128]
            rows = slice((2 - si) * 256, (3 - si) * 256)
            partial[2 - kb, rows, :] = tap if i == 0 else partial[2 - kb, rows, :] + tap

    def convolve(kb, first, n):
        piece = fim[kb * ROWS + first : kb * ROWS + first + n].reshape(n * 160, 768)
        return jnp.dot(piece, w[kb].reshape(768, 128), preferred_element_type=jnp.float32)

    def input_gradient(i):
        n = 4
        piece = jnp.concatenate(
            [gim[kb * ROWS + n * i : kb * ROWS + n * (i + 1)].reshape(n * 160, 384) for kb in range(3)], axis=1
        )
        grad = lax.dot_general(piece, w9[...], (((1,), (1,)), ((), ())), preferred_element_type=jnp.float32)
        back[n * i : n * (i + 1)] = grad.astype(back.dtype).reshape(n, 160, 256)

    def features_taken(j):
        f.take(0, j)
        f.take(1, j)

    def features_used(j):
        n, first = f.sizes[j], f.starts[j]
        f.took(0, j)
        f.took(1, j)
        f.unfold(fim, first, n, above)
        f.unfold(fim, 2 * ROWS + first, n, below)
        at = first * 160
        value = acc[at : at + n * 160, :] + convolve(0, first, n) + convolve(2, first, n)
        out[first : first + n] = value.astype(out.dtype).reshape(n, 160, 128)

    def cotangent_used(i):
        for way, kb, inside in ((0, 0, above), (1, 2, below)):
            g.took(way, i)
            g.unfold(gim, kb * ROWS + 4 * i, 4, inside)
            kernel_gradient(kb, i)
            if i == len(G_SIZES) - 1:
                red[2 - kb].to_core()

    def cotangent_taken(i):
        g.take(0, i)
        g.take(1, i)

    g.strip(0).wait_recv()
    g.strip(1).wait_recv()
    g.unfold(gim, ROWS, ROWS)
    for i in range(3):
        kernel_gradient(1, i)
    red[1].to_core()
    f.strip(0).wait_recv()
    f.strip(1).wait_recv()
    f.unfold(fim, ROWS, ROWS)
    acc[0:640, :] = convolve(1, 0, 4)
    red[1].to_first()
    cotangent_taken(0)
    acc[640:1280, :] = convolve(1, 4, 4)
    acc[1280:1920, :] = convolve(1, 8, 4)
    cotangent_taken(1)
    cotangent_used(0)
    red[1].to_second()
    cotangent_used(1)
    cotangent_taken(2)
    cotangent_used(2)
    red[1].to_y()
    f.send(1)
    input_gradient(0)
    red[2].to_first()
    red[0].to_first()
    features_taken(0)
    red[1].gather_parts(scale)
    input_gradient(1)
    features_used(0)
    red[2].to_second()
    red[0].to_second()
    f.send(2)
    red[1].gather_whole()
    features_taken(1)
    input_gradient(2)
    features_used(1)
    red[2].to_y()
    red[0].to_y()
    f.send(3)
    features_taken(2)
    red[1].gather_core()
    features_used(2)
    red[2].gather_parts(scale)
    red[0].gather_parts(scale)
    f.send(4)
    features_taken(3)
    features_used(3)
    red[2].gather_whole()
    red[0].gather_whole()
    features_taken(4)
    red[2].gather_core()
    red[0].gather_core()
    features_used(4)
    for k in (1, 2, 0):
        red[k].finish()
    for k in (1, 2, 0):
        red[k].drain()
    g.drain()
    f.drain()


def body(features, weight, cotangent):
    bf16, f32 = jnp.bfloat16, jnp.float32
    dma = pltpu.SemaphoreType.DMA
    pixels = ROWS * BLOCKS * 160 * COLS
    anywhere = pl.BlockSpec(memory_space=pl.ANY)
    vmem = pl.BlockSpec(memory_space=pltpu.VMEM)
    conv_out, input_grad, weight_grad = pl.pallas_call(
        functools.partial(branch_kernel, float(pixels) ** -0.5),
        out_shape=(
            jax.ShapeDtypeStruct((ROWS, 160, 128), bf16),
            jax.ShapeDtypeStruct((ROWS, 160, 256), bf16),
            jax.ShapeDtypeStruct((3, 768, 128), f32),
        ),
        in_specs=[anywhere] * 3,
        out_specs=(vmem, vmem, vmem),
        scratch_shapes=[
            pltpu.VMEM((3 * ROWS, 192, 256), bf16),
            pltpu.VMEM((3 * ROWS, 192, 128), bf16),
            pltpu.VMEM((3 * ROWS, 160, 768), bf16),
            pltpu.VMEM((3 * ROWS, 160, 384), bf16),
            pltpu.VMEM((256, ROWS * 160), bf16),
            pltpu.VMEM((3, 3, 256, 128), bf16),
            pltpu.VMEM((256, 1152), bf16),
            pltpu.VMEM((ROWS * 160, 128), f32),
            pltpu.VMEM((3, 768, 128), f32),
            dma((3,)),
            dma((2, 2)),
            dma((2, 2, len(F_SIZES))),
            dma((2, 2, 2, len(F_SIZES))),
            dma((2, 2)),
            dma((2, 2, len(G_SIZES))),
            dma((2, 2, 2, len(G_SIZES))),
        ]
        + reduction_scratch(3),
        compiler_params=pltpu.CompilerParams(collective_id=0, has_side_effects=True, vmem_limit_bytes=VMEM_BYTES),
        name="branch_kernel",
    )(features, weight, cotangent)
    return conv_out, input_grad, weight_grad.reshape(weight.shape)


def solution(mesh):
    placed = (P("rows", "cols", None), P(), P("rows", "cols", None))
    return jax.shard_map(
        body,
        mesh=mesh,
        in_specs=placed,
        out_specs=(P("rows", "cols", None), P("rows", "cols", None), P()),
        check_vma=False,
    )
```

time: 85.7 us -> 73.7 us (0.86)
  Pallas kernels: 80.3 us -> 66.5 us
  local copies, waits for them, and re-layouts: 4.57 us -> 6.03 us
    pallas_call x1, Pallas kernels: 80.3 us -> 66.5 us  [body(): pl.pallas_call(functools.partial(branch_kernel, float(pixels) ** (-0.5)),...]
    unnamed x7 -> x9, local copies, waits for them, and re-layouts: 4.57 us -> 6.03 us
where the time goes in v3:
time: 73.7 us; the launch traced here: 73.2 us
  Pallas kernels  66.5 us (90%)
  local copies, waits for them, and re-layouts  6.03 us (8%)
    pallas_call x1, Pallas kernels, body(): pl.pallas_call(functools.partial(branch_kernel, float(pixels) ** (-0.5)),...  66.5 us
    unnamed x9, local copies, waits for them, and re-layouts  6.03 us

profile of v3, /device:TPU:1, one launch (start us, length us, event | category | flops | bytes accessed | tf_op | source)
XLA Modules:
  0.0 73.2 jit_solution(5246663420930094047)
XLA Ops:
  0.6 0.0 copy-start
  0.6 1.2 %copy-done = bf16[12,160,256]{2,1,0:T(8,128)(2,1)S(1)} copy-done((bf16[12,160,256]{2,1,0:T(8,128)(2,1)S(1)}, bf16[12,160,256]{2,1,0:T(8,128)(2,1)}, u32[]{:S(2)}) %copy-start) | copy-done | bytes 983064
  1.8 0.0 copy-start.1
  1.8 1.1 %copy-done.1 = bf16[3,3,256,128]{3,2,1,0:T(8,128)(2,1)S(1)} copy-done((bf16[3,3,256,128]{3,2,1,0:T(8,128)(2,1)S(1)}, bf16[3,3,256,128]{3,2,1,0:T(8,128)(2,1)}, u32[]{:S(2)}) %copy-start.1) | copy-done | bytes 589848
  2.9 0.0 copy-start.2
  2.9 1.0 %copy-done.2 = bf16[12,160,128]{2,1,0:T(8,128)(2,1)S(1)} copy-done((bf16[12,160,128]{2,1,0:T(8,128)(2,1)S(1)}, bf16[12,160,128]{2,1,0:T(8,128)(2,1)}, u32[]{:S(2)}) %copy-start.2) | copy-done | bytes 491544
  3.9 66.5 %branch_kernel.1 = (bf16[12,160,128]{2,1,0:T(8,128)(2,1)S(1)}, bf16[12,160,256]{2,1,0:T(8,128)(2,1)S(1)}, f32[3,768,128]{2,1,0:T(8,128)S(1)}) custom-call(bf16[12,160,256]{2,1,0:T(8,128)(2,1)S(1)} %copy-done, bf16[3,3,256,128]{3,2,1,0:T(8,128)(2,1)S(1)} %copy-done.1, bf16[12,160,128]{2,1,0:T(8,128)(2,1)S(1)} %copy-done.2), custom_call_target="tpu_custom_call" | custom-call | tf_op jit(solution)/shard_map/branch_kernel/pallas_call | solution.py:495
  70.4 0.8 %copy.9 = bf16[12,160,128]{2,1,0:T(8,128)(2,1)} copy(bf16[12,160,128]{2,1,0:T(8,128)(2,1)S(1)} %get-tuple-element.12) | data formatting | bytes 983040
  71.2 0.9 %copy.10 = bf16[12,160,256]{2,1,0:T(8,128)(2,1)} copy(bf16[12,160,256]{2,1,0:T(8,128)(2,1)S(1)} %get-tuple-element.13) | data formatting | bytes 1966080
  72.2 1.0 %copy.11 = f32[3,3,256,128]{3,2,1,0:T(8,128)} copy(f32[3,3,256,128]{3,2,1,0:T(8,128)S(1)} %bitcast.1) | data formatting | bytes 2359296
Async XLA Ops:
  0.6 1.2 %copy-start = (bf16[12,160,256]{2,1,0:T(8,128)(2,1)S(1)}, bf16[12,160,256]{2,1,0:T(8,128)(2,1)}, u32[]{:S(2)}) copy-start(bf16[12,160,256]{2,1,0:T(8,128)(2,1)} %f_hbm.1) | copy-start | bytes 2949124
  1.8 1.1 %copy-start.1 = (bf16[3,3,256,128]{3,2,1,0:T(8,128)(2,1)S(1)}, bf16[3,3,256,128]{3,2,1,0:T(8,128)(2,1)}, u32[]{:S(2)}) copy-start(bf16[3,3,256,128]{3,2,1,0:T(8,128)(2,1)} %w_hbm.1) | copy-start | bytes 1769476
  2.9 1.0 %copy-start.2 = (bf16[12,160,128]{2,1,0:T(8,128)(2,1)S(1)}, bf16[12,160,128]{2,1,0:T(8,128)(2,1)}, u32[]{:S(2)}) copy-start(bf16[12,160,128]{2,1,0:T(8,128)(2,1)} %g_hbm.1) | copy-start | bytes 1474564

commit v4 on v3

--- a/solution.py
+++ b/solution.py
@@ -486,6 +486,27 @@
     f.drain()
 
 
+def store_kernel(a, b, c, a_out, b_out, c_out, sem):
+    copies = [pltpu.make_async_copy(src, dst, sem.at[i]) for i, (src, dst) in enumerate(((c, c_out), (b, b_out), (a, a_out)))]
+    for copy in copies:
+        copy.start()
+    for copy in copies:
+        copy.wait()
+
+
+def stored(arrays):
+    anywhere = pl.BlockSpec(memory_space=pl.ANY)
+    return pl.pallas_call(
+        store_kernel,
+        out_shape=tuple(jax.ShapeDtypeStruct(x.shape, x.dtype) for x in arrays),
+        in_specs=[anywhere] * 3,
+        out_specs=(anywhere,) * 3,
+        scratch_shapes=[pltpu.SemaphoreType.DMA((3,))],
+        compiler_params=pltpu.CompilerParams(vmem_limit_bytes=1024 * 1024),
+        name="store_kernel",
+    )(*arrays)
+
+
 def body(features, weight, cotangent):
     bf16, f32 = jnp.bfloat16, jnp.float32
     dma = pltpu.SemaphoreType.DMA
@@ -522,7 +543,8 @@
         + reduction_scratch(3),
         compiler_params=pltpu.CompilerParams(collective_id=0, has_side_effects=True, vmem_limit_bytes=VMEM_BYTES),
         name="branch_kernel",
-    )(features, weight, cotangent)
+    )(*(pltpu.with_memory_space_constraint(x, pltpu.HBM) for x in (features, weight, cotangent)))
+    conv_out, input_grad, weight_grad = stored((conv_out, input_grad, weight_grad))
     return conv_out, input_grad, weight_grad.reshape(weight.shape)
 
 

time: 73.7 us -> 68.9 us (0.935)
  local copies, waits for them, and re-layouts: 6.03 us -> 0 us
  Pallas kernels: 66.5 us -> 67.8 us
    unnamed x9 -> x0, local copies, waits for them, and re-layouts: 6.03 us -> none
    pallas_call x0 -> x1, Pallas kernels: none -> 1.52 us  [stored(): pl.pallas_call(store_kernel, out_shape=tuple((jax.ShapeDtypeStruct(x.shap...]
where the time goes in v4:
time: 68.9 us; the launch traced here: 68.5 us
  Pallas kernels  67.8 us (98%)
    pallas_call x1, Pallas kernels, body(): pl.pallas_call(functools.partial(branch_kernel, float(pixels) ** (-0.5)),...  66.3 us
    pallas_call x1, Pallas kernels, stored(): pl.pallas_call(store_kernel, out_shape=tuple((jax.ShapeDtypeStruct(x.shap...  1.52 us

profile of v4, /device:TPU:1, one launch (start us, length us, event | category | flops | bytes accessed | tf_op | source)
XLA Modules:
  0.0 68.5 jit_solution(12238713019230033315)
XLA Ops:
  0.6 66.3 %branch_kernel.1 = (bf16[12,160,128]{2,1,0:T(8,128)(2,1)S(1)}, bf16[12,160,256]{2,1,0:T(8,128)(2,1)S(1)}, f32[3,768,128]{2,1,0:T(8,128)S(1)}) custom-call(bf16[12,160,256]{2,1,0:T(8,128)(2,1)} %f_hbm.1, bf16[3,3,256,128]{3,2,1,0:T(8,128)(2,1)} %w_hbm.1, bf16[12,160,128]{2,1,0:T(8,128)(2,1)} %g_hbm.1), custom_call_target="tpu_custom_call" | custom-call | tf_op jit(solution)/shard_map/branch_kernel/pallas_call | solution.py:516
  66.9 1.5 %store_kernel.1 = (bf16[12,160,128]{2,1,0:T(8,128)(2,1)}, bf16[12,160,256]{2,1,0:T(8,128)(2,1)}, f32[3,768,128]{2,1,0:T(8,128)}) custom-call(bf16[12,160,128]{2,1,0:T(8,128)(2,1)S(1)} %get-tuple-element.9.a, bf16[12,160,256]{2,1,0:T(8,128)(2,1)S(1)} %get-tuple-element.10.b, f32[3,768,128]{2,1,0:T(8,128)S(1)} %get-tuple-element.11.c), custom_call_target="tpu_custom_call" | custom-call | tf_op jit(solution)/shard_map/store_kernel/pallas_call | solution.py:499

commit v5 on v4

--- a/solution.py
+++ b/solution.py
@@ -9,8 +9,8 @@
 
 ROWS = 12
 BLOCKS, COLS = 32, 8
-G_SIZES, F_SIZES = (4, 4, 4), (2, 3, 2, 2, 3)
-G_DIRECT, F_DIRECT = 1, 0
+G_SIZES, F_SIZES = (4, 4, 4), (2, 4, 1, 2, 3)
+G_DIRECT, F_DIRECT = 1, 1
 VMEM_BYTES = 36 * 1024 * 1024
 MESH = pl.DeviceIdType.MESH
 NX, NY, NZ = 4, 4, 8
@@ -34,7 +34,7 @@
     def __init__(self, piece, order, where, partial, total, scratch):
         self.k = piece
         self.row, self.col, self.x, self.core, self.y, self.z = where
-        (self.half, self.s1, self.first, self.s2, self.second, self.ys, self.parts, self.near, self.first_sem, self.second_sem,
+        (self.half, self.s1, self.first, self.s2, self.second, self.ys, self.near, self.first_sem, self.second_sem,
          self.ysem, self.parts_sem, self.whole_sem, self.far_sem) = scratch
         self.partial, self.total = partial, total
         self.order = order
@@ -81,9 +81,33 @@
     def y_copy(self, d):
         return self.copy(self.ys.at[self.k, self.y], self.ys.at[self.k, self.y], self.ysem, d - 1, self.along("y", d))
 
-    def part_copy(self, d):
-        here = self.parts.at[self.k, self.i2]
-        return self.copy(here, here, self.parts_sem, d - 1, self.along(self.order[1], d))
+    def parity(self, z, body):
+        even = lax.rem(z, 2) == 0
+        pl.when(even)(lambda: body(0, 16))
+        pl.when(jnp.logical_not(even))(lambda: body(16, 8))
+
+    def part_of(self, z, start, size):
+        base = self.core * HALF + self.i1 * self.shard + lax.div(z, 2) * 24
+        return self.total.at[self.k, rows_at(base + start, size)]
+
+    def part_copies(self, d, act):
+        def go(start, size):
+            here = self.part_of(self.i2, start, size)
+            act(self.copy(here, here, self.parts_sem, d - 1, self.along("z", d)))
+
+        self.parity(self.i2, go)
+
+    def take_part(self, d):
+        source = lax.rem(self.i2 + NZ - d, NZ)
+
+        def go(start, size):
+            here = self.part_of(source, start, size)
+            if not isinstance(d, int) or d:
+                self.copy(here, here, self.parts_sem, d - 1, self.along("z", d)).wait_recv()
+            for step in (2, 1, 3):
+                self.copy(here, here, self.whole_sem, step - 1, self.along("x", step)).start()
+
+        self.parity(source, go)
 
     def span(self, i):
         return self.total.at[self.k, rows_at(self.core * HALF + i * self.shard, self.shard)]
@@ -140,17 +164,19 @@
         k = self.k
         for d in range(1, NY):
             self.y_copy(d).wait_recv()
-        self.parts[k, self.i2] = (self.ys[k, 0] + self.ys[k, 1] + self.ys[k, 2] + self.ys[k, 3]) * scale
-        self.loop(self.n2, lambda d: self.part_copy(d).start())
+        mine = (self.ys[k, 0] + self.ys[k, 1] + self.ys[k, 2] + self.ys[k, 3]) * scale
+        base = self.core * HALF + self.i1 * self.shard + lax.div(self.i2, 2) * 24
+
+        def keep(start, size):
+            self.total[k, rows_at(base + start, size)] = mine[16 - size :]
+
+        self.parity(self.i2, keep)
+        self.loop(NZ, lambda d: self.part_copies(d, lambda copy: copy.start()))
+        self.take_part(0)
 
     def gather_whole(self):
-        k = self.k
-        self.loop(self.n2, lambda d: self.part_copy(d).wait_recv())
-        base = self.core * HALF + self.i1 * self.shard
-        for pair in range(self.n2 // 2):
-            self.total[k, rows_at(base + 24 * pair, 16)] = self.parts[k, 2 * pair]
-            self.total[k, rows_at(base + 24 * pair + 16, 8)] = self.parts[k, 2 * pair + 1, 8:16]
-        self.loop(self.n1, lambda d: self.whole_copy(d).start())
+        for d in (1, 7, 2, 6, 3, 5, 4):
+            self.take_part(d)
         self.far_copy(0).start()
 
     def gather_core(self):
@@ -168,7 +194,7 @@
         self.loop(self.n1, lambda d: self.first_copy(d).wait_send())
         self.loop(self.n1, lambda d: self.whole_copy(d).wait_send())
         self.loop(self.n2, lambda d: self.second_copy(d).wait_send())
-        self.loop(self.n2, lambda d: self.part_copy(d).wait_send())
+        self.loop(NZ, lambda d: self.part_copies(d, lambda copy: copy.wait_send()))
         for d in range(1, NY):
             self.y_copy(d).wait_send()
         self.loop(self.n1, lambda d: self.far_copy(d).wait_send(), 0)
@@ -185,7 +211,6 @@
         pltpu.VMEM((pieces, HALF // NX, 128), f32),
         pltpu.VMEM((pieces, most - 1, PART, 128), f32),
         pltpu.VMEM((pieces, NY, PART, 128), f32),
-        pltpu.VMEM((pieces, most, PART, 128), f32),
         dma((2, pieces, 1)),
         dma((2, pieces, most - 1)),
         dma((2, pieces, most - 1)),
@@ -470,10 +495,16 @@
     red[2].gather_parts(scale)
     red[0].gather_parts(scale)
     f.send(4)
+    for d in (1, 7, 2, 6):
+        red[2].take_part(d)
+        red[0].take_part(d)
     features_taken(3)
+    for d in (3, 5, 4):
+        red[2].take_part(d)
+        red[0].take_part(d)
+    red[2].far_copy(0).start()
+    red[0].far_copy(0).start()
     features_used(3)
-    red[2].gather_whole()
-    red[0].gather_whole()
     features_taken(4)
     red[2].gather_core()
     red[0].gather_core()

time: 68.9 us -> 67.5 us (0.980)
  Pallas kernels: 67.8 us -> 66.8 us
    pallas_call x1, Pallas kernels: 66.3 us -> 65.2 us  [body(): pl.pallas_call(functools.partial(branch_kernel, float(pixels) ** (-0.5)),...]
where the time goes in v5:
time: 67.5 us; the launch traced here: 67.4 us
  Pallas kernels  66.8 us (99%)
    pallas_call x1, Pallas kernels, body(): pl.pallas_call(functools.partial(branch_kernel, float(pixels) ** (-0.5)),...  65.2 us
    pallas_call x1, Pallas kernels, stored(): pl.pallas_call(store_kernel, out_shape=tuple((jax.ShapeDtypeStruct(x.shap...  1.52 us

profile of v5, /device:TPU:1, one launch (start us, length us, event | category | flops | bytes accessed | tf_op | source)
XLA Modules:
  0.0 67.4 jit_solution(18362894110350222016)
XLA Ops:
  0.6 65.2 %branch_kernel.1 = (bf16[12,160,128]{2,1,0:T(8,128)(2,1)S(1)}, bf16[12,160,256]{2,1,0:T(8,128)(2,1)S(1)}, f32[3,768,128]{2,1,0:T(8,128)S(1)}) custom-call(bf16[12,160,256]{2,1,0:T(8,128)(2,1)} %f_hbm.1, bf16[3,3,256,128]{3,2,1,0:T(8,128)(2,1)} %w_hbm.1, bf16[12,160,128]{2,1,0:T(8,128)(2,1)} %g_hbm.1), custom_call_target="tpu_custom_call" | custom-call | tf_op jit(solution)/shard_map/branch_kernel/pallas_call | solution.py:547
  65.9 1.5 %store_kernel.1 = (bf16[12,160,128]{2,1,0:T(8,128)(2,1)}, bf16[12,160,256]{2,1,0:T(8,128)(2,1)}, f32[3,768,128]{2,1,0:T(8,128)}) custom-call(bf16[12,160,128]{2,1,0:T(8,128)(2,1)S(1)} %get-tuple-element.9.a, bf16[12,160,256]{2,1,0:T(8,128)(2,1)S(1)} %get-tuple-element.10.b, f32[3,768,128]{2,1,0:T(8,128)S(1)} %get-tuple-element.11.c), custom_call_target="tpu_custom_call" | custom-call | tf_op jit(solution)/shard_map/store_kernel/pallas_call | solution.py:530

commit v6 on v5

--- a/solution.py
+++ b/solution.py
@@ -9,7 +9,7 @@
 
 ROWS = 12
 BLOCKS, COLS = 32, 8
-G_SIZES, F_SIZES = (4, 4, 4), (2, 4, 1, 2, 3)
+G_SIZES, F_SIZES = (4, 4, 4), (2, 4, 1, 2, 2, 1)
 G_DIRECT, F_DIRECT = 1, 1
 VMEM_BYTES = 36 * 1024 * 1024
 MESH = pl.DeviceIdType.MESH
@@ -104,7 +104,7 @@
             here = self.part_of(source, start, size)
             if not isinstance(d, int) or d:
                 self.copy(here, here, self.parts_sem, d - 1, self.along("z", d)).wait_recv()
-            for step in (2, 1, 3):
+            for step in (1, 3, 2):
                 self.copy(here, here, self.whole_sem, step - 1, self.along("x", step)).start()
 
         self.parity(source, go)
@@ -495,6 +495,7 @@
     red[2].gather_parts(scale)
     red[0].gather_parts(scale)
     f.send(4)
+    f.send(5)
     for d in (1, 7, 2, 6):
         red[2].take_part(d)
         red[0].take_part(d)
@@ -509,6 +510,8 @@
     red[2].gather_core()
     red[0].gather_core()
     features_used(4)
+    features_taken(5)
+    features_used(5)
     for k in (1, 2, 0):
         red[k].finish()
     for k in (1, 2, 0):

time: 67.5 us -> 67.1 us (level)
  no operation moved by 1% of the time
where the time goes in v6:
time: 67.1 us; the launch traced here: 67 us
  Pallas kernels  66.4 us (99%)
    pallas_call x1, Pallas kernels, body(): pl.pallas_call(functools.partial(branch_kernel, float(pixels) ** (-0.5)),...  64.9 us
    pallas_call x1, Pallas kernels, stored(): pl.pallas_call(store_kernel, out_shape=tuple((jax.ShapeDtypeStruct(x.shap...  1.52 us

profile of v6, /device:TPU:1, one launch (start us, length us, event | category | flops | bytes accessed | tf_op | source)
XLA Modules:
  0.0 67.0 jit_solution(13307936794215611402)
XLA Ops:
  0.6 64.9 %branch_kernel.1 = (bf16[12,160,128]{2,1,0:T(8,128)(2,1)S(1)}, bf16[12,160,256]{2,1,0:T(8,128)(2,1)S(1)}, f32[3,768,128]{2,1,0:T(8,128)S(1)}) custom-call(bf16[12,160,256]{2,1,0:T(8,128)(2,1)} %f_hbm.1, bf16[3,3,256,128]{3,2,1,0:T(8,128)(2,1)} %w_hbm.1, bf16[12,160,128]{2,1,0:T(8,128)(2,1)} %g_hbm.1), custom_call_target="tpu_custom_call" | custom-call | tf_op jit(solution)/shard_map/branch_kernel/pallas_call | solution.py:550
  65.5 1.5 %store_kernel.1 = (bf16[12,160,128]{2,1,0:T(8,128)(2,1)}, bf16[12,160,256]{2,1,0:T(8,128)(2,1)}, f32[3,768,128]{2,1,0:T(8,128)}) custom-call(bf16[12,160,128]{2,1,0:T(8,128)(2,1)S(1)} %get-tuple-element.9.a, bf16[12,160,256]{2,1,0:T(8,128)(2,1)S(1)} %get-tuple-element.10.b, f32[3,768,128]{2,1,0:T(8,128)S(1)} %get-tuple-element.11.c), custom_call_target="tpu_custom_call" | custom-call | tf_op jit(solution)/shard_map/store_kernel/pallas_call | solution.py:533

commit v7 on v6

--- a/solution.py
+++ b/solution.py
@@ -9,7 +9,7 @@
 
 ROWS = 12
 BLOCKS, COLS = 32, 8
-G_SIZES, F_SIZES = (4, 4, 4), (2, 4, 1, 2, 2, 1)
+G_SIZES, F_SIZES = (4, 4, 4), (2, 4, 2, 2, 1, 1)
 G_DIRECT, F_DIRECT = 1, 1
 VMEM_BYTES = 36 * 1024 * 1024
 MESH = pl.DeviceIdType.MESH

time: 67.1 us -> 68.2 us (1.016)
  Pallas kernels: 66.4 us -> 67.5 us
    pallas_call x1, Pallas kernels: 64.9 us -> 65.9 us  [body(): pl.pallas_call(functools.partial(branch_kernel, float(pixels) ** (-0.5)),...]
where the time goes in v7:
time: 68.2 us; the launch traced here: 68.1 us
  Pallas kernels  67.5 us (99%)
    pallas_call x1, Pallas kernels, body(): pl.pallas_call(functools.partial(branch_kernel, float(pixels) ** (-0.5)),...  65.9 us
    pallas_call x1, Pallas kernels, stored(): pl.pallas_call(store_kernel, out_shape=tuple((jax.ShapeDtypeStruct(x.shap...  1.52 us

profile of v7, /device:TPU:1, one launch (start us, length us, event | category | flops | bytes accessed | tf_op | source)
XLA Modules:
  0.0 68.1 jit_solution(15004610099425004725)
XLA Ops:
  0.6 65.9 %branch_kernel.1 = (bf16[12,160,128]{2,1,0:T(8,128)(2,1)S(1)}, bf16[12,160,256]{2,1,0:T(8,128)(2,1)S(1)}, f32[3,768,128]{2,1,0:T(8,128)S(1)}) custom-call(bf16[12,160,256]{2,1,0:T(8,128)(2,1)} %f_hbm.1, bf16[3,3,256,128]{3,2,1,0:T(8,128)(2,1)} %w_hbm.1, bf16[12,160,128]{2,1,0:T(8,128)(2,1)} %g_hbm.1), custom_call_target="tpu_custom_call" | custom-call | tf_op jit(solution)/shard_map/branch_kernel/pallas_call | solution.py:550
  66.6 1.5 %store_kernel.1 = (bf16[12,160,128]{2,1,0:T(8,128)(2,1)}, bf16[12,160,256]{2,1,0:T(8,128)(2,1)}, f32[3,768,128]{2,1,0:T(8,128)}) custom-call(bf16[12,160,128]{2,1,0:T(8,128)(2,1)S(1)} %get-tuple-element.9.a, bf16[12,160,256]{2,1,0:T(8,128)(2,1)S(1)} %get-tuple-element.10.b, f32[3,768,128]{2,1,0:T(8,128)S(1)} %get-tuple-element.11.c), custom_call_target="tpu_custom_call" | custom-call | tf_op jit(solution)/shard_map/store_kernel/pallas_call | solution.py:533
